TPU v7x, 256 devices: a whole 4x4x8 slice. The times are simulated.
256 devices in a mesh: modes: 64 (over y, x, z_hi), mom: 4 (over z_lo, core).
Axes of the slice: x: 4, y: 4, z: 8 (z_hi: 4, z_lo: 2; z = z_hi * 2 + z_lo), core: 2. Of those that a mesh axis runs over, the one named last changes fastest.
Arguments:
- elementals: float32 [2, 8, 256, 256, 256], P(None, 'mom', 'modes'), parts along dimension 1, may hold values from -64 to 64
- perambulators: float32 [64, 2, 2, 256, 256], P('modes'), may hold values from -0.25 to 0.25
- owners: int32 [2], replicated, may hold values from 0 to 63
- pairing: int32 [8], P('mom'), parts along dimension 0, may hold values from 0 to 1
Outputs:
- propagated: bfloat16 [2, 8, 2, 256, 256, 256], P(None, 'mom', None, 'modes'), parts along dimension 1
- correlator: float32 [2, 8, 2], P(None, 'mom'), parts along dimension 1
There are 4 independent parts, one for each index of `mom`. A program takes and returns all parts, laid end to end along the dimension named above; an argument that names none is the same for every part. Nothing has to cross between parts.
All inputs are finite; a program needn't handle non-finite values.
Results may differ from a plain program's by a relative error of at most 0.001.
Values sent between devices are 32-bit elements; how exact they have to be, the bound alone decides.
No kernel may reach another device: no remote copies, remote signals or barrier semaphores. Data moves between devices by JAX's collectives and lax.ppermute only.
A program may use at most 128 MiB of HBM per device.

v0:
```python
import jax
import jax.numpy as jnp
from jax import lax
from jax.sharding import PartitionSpec as P

N = 256


highest = lax.Precision.HIGHEST


def spread(block, axis, source):
    block = jnp.where(lax.axis_index(axis) == source, block, jnp.zeros_like(block))
    return lax.psum(block, axis)


def complex_product(formula, matrix_re, matrix_im, tensor_re, tensor_im):

    def single(left_part, right_part):
        return jnp.einsum(formula, left_part, right_part, precision=highest)

    real_part = single(matrix_re, tensor_re) - single(matrix_im, tensor_im)
    imag_part = single(matrix_re, tensor_im) + single(matrix_im, tensor_re)
    return (real_part, imag_part)


def local_pair(elem_re, elem_im, peram_re, peram_im):
    third_re, third_im = complex_product("kc,abc->abk", peram_re, peram_im, elem_re, elem_im)
    result = complex_product("jb,abk->kaj", peram_re, peram_im, third_re, third_im)
    return result


def shards(elementals, perambulators, owners, pairing):
    mom_count = elementals.shape[1]
    time_count = perambulators.shape[1]
    norm_scale = float(N) ** (-1.5)
    perams = []
    for time_index in range(time_count):
        perams.append(spread(perambulators[0, time_index], "modes", owners[time_index]))
    sink_slabs = []
    for mom_index in range(mom_count):
        picked = lax.dynamic_index_in_dim(elementals, pairing[mom_index], 1, keepdims=False)
        sink_slabs.append((jnp.swapaxes(picked[0], 1, 2), jnp.swapaxes(picked[1], 1, 2)))
    carried_re = [[None] * time_count for mom_index in range(mom_count)]
    carried_im = [[None] * time_count for mom_index in range(mom_count)]
    sums_real = [[None] * time_count for mom_index in range(mom_count)]
    sums_imag = [[None] * time_count for mom_index in range(mom_count)]
    for time_index in range(time_count):
        peram_re = perams[time_index][0]
        peram_im = perams[time_index][1]
        outputs = []
        for mom_index in range(mom_count):
            slab_re, slab_im = local_pair(
                elementals[0, mom_index], elementals[1, mom_index], peram_re, peram_im
            )
            outputs.append(
                complex_product(
                    "ia,kaj->kij",
                    peram_re,
                    peram_im,
                    lax.all_to_all(slab_re, "modes", split_axis=0, concat_axis=1, tiled=True),
                    lax.all_to_all(slab_im, "modes", split_axis=0, concat_axis=1, tiled=True),
                )
            )
        for mom_index in range(mom_count):
            out_re, out_im = outputs[mom_index]
            sink_re, sink_im = sink_slabs[mom_index]
            sums_real[mom_index][time_index] = jnp.sum(sink_re * out_re + sink_im * out_im)
            sums_imag[mom_index][time_index] = jnp.sum(sink_re * out_im - sink_im * out_re)
            carried_re[mom_index][time_index] = out_re
            carried_im[mom_index][time_index] = out_im
    partial_sums = jnp.stack(
        [
            jnp.stack([jnp.stack(row) for row in sums_real]),
            jnp.stack([jnp.stack(row) for row in sums_imag]),
        ]
    )
    correlator = lax.psum(partial_sums, "modes") * norm_scale
    propagated = jnp.stack(
        [
            jnp.stack([jnp.stack(row) for row in carried_re]),
            jnp.stack([jnp.stack(row) for row in carried_im]),
        ]
    ).astype(jnp.bfloat16)
    return (propagated, correlator)


def solution(mesh):
    placed = (
        P(None, "mom", "modes", None, None),
        P("modes", None, None, None, None),
        P(),
        P("mom"),
    )
    return jax.shard_map(
        shards,
        mesh=mesh,
        in_specs=placed,
        out_specs=(P(None, "mom", None, "modes", None, None), P(None, "mom", None)),
        check_vma=False,
    )
```

profile of v0, /device:TPU:32, one launch (start us, length us, event | category | flops | bytes accessed | tf_op | source)
XLA Modules:
  0.0 1280.3 jit_solution(18263410880325923134)
XLA Ops:
  9.8 2.3 select_bitcast_fusion.1
  12.1 742.1 %all-reduce.3.cloned.1.call-done = (f32[2,256,256]{2,1,0:T(8,128)}, f32[2,256,256]{2,1,0:T(8,128)}) async-done(((f32[2,256,256]{2,1,0:T(8,128)}, f32[2,256,256]{2,1,0:T(8,128)}), (f32[2,256,256]{2,1,0:T(8,128)}, f32[2,256,256]{2,1,0:T(8,128)})) %all-reduce.3.cloned.1.call-update) | async-done | bytes 1048592 | tf_op jit(solution)/shard_map/psum | solution.py:14
  754.3 2.5 fusion.23
  756.8 2.4 fusion.16
  765.0 9.8 all-to-all-start.6
  778.5 27.7 %all-to-all-done.6 = f32[256,4,256]{2,1,0:T(4,128)} async-done(((f32[256,4,256]{2,1,0:T(4,128)}), f32[256,4,256]{2,1,0:T(4,128)}, u32[]{:S(2)}, u32[]{:S(2)}) %all-to-all-start.6) | async-done | bytes 1048608 | tf_op jit(solution)/shard_map/all_to_all | solution.py:61
  806.2 6.6 all-to-all-start.7
  812.8 2.4 fusion.28
  815.2 2.3 fusion.35
  823.4 18.2 %all-to-all-done.7 = f32[256,4,256]{2,1,0:T(4,128)} async-done(((f32[256,4,256]{2,1,0:T(4,128)}), f32[256,4,256]{2,1,0:T(4,128)}, u32[]{:S(2)}, u32[]{:S(2)}) %all-to-all-start.7) | async-done | bytes 1048608 | tf_op jit(solution)/shard_map/all_to_all | solution.py:62
  841.6 5.5 all-to-all-start.3
  850.8 24.3 %all-to-all-done.3 = f32[256,4,256]{2,1,0:T(4,128)} async-done(((f32[256,4,256]{2,1,0:T(4,128)}), f32[256,4,256]{2,1,0:T(4,128)}, u32[]{:S(2)}, u32[]{:S(2)}) %all-to-all-start.3) | async-done | bytes 1048608 | tf_op jit(solution)/shard_map/all_to_all | solution.py:62
  875.1 6.5 all-to-all-start.2
  881.6 2.4 fusion.26
  884.0 2.3 fusion.19
  892.1 14.7 %all-to-all-done.2 = f32[256,4,256]{2,1,0:T(4,128)} async-done(((f32[256,4,256]{2,1,0:T(4,128)}), f32[256,4,256]{2,1,0:T(4,128)}, u32[]{:S(2)}, u32[]{:S(2)}) %all-to-all-start.2) | async-done | bytes 1048608 | tf_op jit(solution)/shard_map/all_to_all | solution.py:61
  906.9 6.5 all-to-all-start.4
  917.1 19.1 %all-to-all-done.4 = f32[256,4,256]{2,1,0:T(4,128)} async-done(((f32[256,4,256]{2,1,0:T(4,128)}), f32[256,4,256]{2,1,0:T(4,128)}, u32[]{:S(2)}, u32[]{:S(2)}) %all-to-all-start.4) | async-done | bytes 1048608 | tf_op jit(solution)/shard_map/all_to_all | solution.py:61
  936.2 6.5 all-to-all-start.5
  942.8 2.4 fusion.31
  945.2 2.3 fusion.38
  953.3 9.2 all-to-all-done.5
  962.5 6.7 all-to-all-start.1
  979.2 2.5 copy.62
  983.3 2.9 copy.50
  986.2 2.6 copy.51
  988.8 2.5 copy.47
  991.3 2.6 copy.48
  993.9 2.5 copy.53
  996.4 2.5 copy.54
  999.0 2.5 copy.56
  1001.5 2.5 copy.57
  1004.1 2.1 fusion.64
  1006.1 2.1 fusion.67
  1010.2 2.0 fusion.65
  1012.2 2.2 fusion.56
  1014.5 12.9 %all-to-all-start = ((f32[256,4,256]{2,1,0:T(4,128)}), f32[256,4,256]{2,1,0:T(4,128)}, u32[]{:S(2)}, u32[]{:S(2)}) async-start(f32[256,4,256]{2,1,0:T(4,128)} %copy.40), calls=%async_computation | async-start | bytes 2097152 | tf_op jit(solution)/shard_map/all_to_all | solution.py:61
  1027.4 2.5 copy.44
  1031.5 2.4 fusion.59
  1033.9 3.3 convolution_add_fusion
  1037.2 2.1 convolution_subtract_fusion
  1047.3 2.5 copy.41
  1054.5 6.6 add_reduce_fusion.3
  1061.1 2.6 maximum_bitcast_fusion.8
  1063.7 2.6 maximum_bitcast_fusion.10
  1066.3 194.2 %psum.23 = f32[2,2,2]{2,1,0:T(2,128)S(1)} all-reduce(f32[2,2,2]{2,1,0:T(2,128)S(1)} %pad_maximum_fusion.1), channel_id=1, replica_groups=mesh['modes'=64,'mom'=4] {'modes'}, use_global_device_ids=true, to_apply=%region_10.11 | all-reduce | flops 8 | bytes 64 | tf_op jit(solution)/shard_map/psum | solution.py:78
  1263.4 2.3 pad_maximum_fusion
  1265.7 7.2 copy.72
  (109 shorter events, 62.6 us)
Async XLA Ops:
  7.2 747.1 %all-reduce.3.cloned.1.call-start = ((), (), s32[]{:S(2)}) async-start(), calls=%async_computation.8 | async-start | bytes 2097152 | tf_op jit(solution)/shard_map/psum | solution.py:14
  754.3 4.9 copy-start
  754.3 4.9 copy-start.6
  765.0 41.2 %all-to-all-start.6 = ((f32[256,4,256]{2,1,0:T(4,128)}), f32[256,4,256]{2,1,0:T(4,128)}, u32[]{:S(2)}, u32[]{:S(2)}) async-start(f32[256,4,256]{2,1,0:T(4,128)} %copy.58), calls=%async_computation.6 | async-start | bytes 2097152 | tf_op jit(solution)/shard_map/all_to_all | solution.py:61
  806.2 35.4 %all-to-all-start.7 = ((f32[256,4,256]{2,1,0:T(4,128)}), f32[256,4,256]{2,1,0:T(4,128)}, u32[]{:S(2)}, u32[]{:S(2)}) async-start(f32[256,4,256]{2,1,0:T(4,128)} %copy.61), calls=%async_computation.7 | async-start | bytes 2097152 | tf_op jit(solution)/shard_map/all_to_all | solution.py:62
  812.8 4.7 copy-start.1
  841.6 33.5 %all-to-all-start.3 = ((f32[256,4,256]{2,1,0:T(4,128)}), f32[256,4,256]{2,1,0:T(4,128)}, u32[]{:S(2)}, u32[]{:S(2)}) async-start(f32[256,4,256]{2,1,0:T(4,128)} %copy.49), calls=%async_computation.3 | async-start | bytes 2097152 | tf_op jit(solution)/shard_map/all_to_all | solution.py:62
  848.1 33.5 %copy-start.5 = (f32[2,256,256]{2,1,0:T(8,128)S(1)}, f32[2,256,256]{2,1,0:T(8,128)}, u32[]{:S(2)}) copy-start(f32[2,256,256]{2,1,0:T(8,128)} %get-tuple-element.23) | copy-start | bytes 1572868
  875.1 31.7 %all-to-all-start.2 = ((f32[256,4,256]{2,1,0:T(4,128)}), f32[256,4,256]{2,1,0:T(4,128)}, u32[]{:S(2)}, u32[]{:S(2)}) async-start(f32[256,4,256]{2,1,0:T(4,128)} %copy.46), calls=%async_computation.2 | async-start | bytes 2097152 | tf_op jit(solution)/shard_map/all_to_all | solution.py:61
  881.6 4.7 copy-start.2
  906.9 29.4 %all-to-all-start.4 = ((f32[256,4,256]{2,1,0:T(4,128)}), f32[256,4,256]{2,1,0:T(4,128)}, u32[]{:S(2)}, u32[]{:S(2)}) async-start(f32[256,4,256]{2,1,0:T(4,128)} %copy.52), calls=%async_computation.4 | async-start | bytes 2097152 | tf_op jit(solution)/shard_map/all_to_all | solution.py:61
  936.2 26.3 %all-to-all-start.5 = ((f32[256,4,256]{2,1,0:T(4,128)}), f32[256,4,256]{2,1,0:T(4,128)}, u32[]{:S(2)}, u32[]{:S(2)}) async-start(f32[256,4,256]{2,1,0:T(4,128)} %copy.55), calls=%async_computation.5 | async-start | bytes 2097152 | tf_op jit(solution)/shard_map/all_to_all | solution.py:62
  942.8 4.7 copy-start.3
  950.6 18.6 %copy-start.24 = (s32[2]{0:T(128)S(1)}, s32[2]{0:T(128)}, u32[]{:S(2)}) copy-start(s32[2]{0:T(128)} %param.7) | copy-start | bytes 28
  962.5 51.9 %all-to-all-start.1 = ((f32[256,4,256]{2,1,0:T(4,128)}), f32[256,4,256]{2,1,0:T(4,128)}, u32[]{:S(2)}, u32[]{:S(2)}) async-start(f32[256,4,256]{2,1,0:T(4,128)} %copy.43), calls=%async_computation.1 | async-start | bytes 2097152 | tf_op jit(solution)/shard_map/all_to_all | solution.py:62
  983.3 20.8 %copy-start.7 = (f32[4,256,256]{1,2,0:T(8,128)}, f32[4,256,256]{1,2,0:T(8,128)S(1)}, u32[]{:S(2)}) copy-start(f32[4,256,256]{1,2,0:T(8,128)S(1)} %copy.63) | copy-start | bytes 3145732
  1004.0 4.1 copy-start.11
  1004.1 6.2 copy-start.9
  1004.1 8.2 copy-start.14
  1014.5 32.8 %all-to-all-start = ((f32[256,4,256]{2,1,0:T(4,128)}), f32[256,4,256]{2,1,0:T(4,128)}, u32[]{:S(2)}, u32[]{:S(2)}) async-start(f32[256,4,256]{2,1,0:T(4,128)} %copy.40), calls=%async_computation | async-start | bytes 2097152 | tf_op jit(solution)/shard_map/all_to_all | solution.py:61
  1031.4 5.7 copy-start.8
  1031.4 5.7 copy-start.22
  1031.4 7.8 copy-start.10
  1031.5 7.8 copy-start.21
  1037.2 4.1 copy-start.12
  1037.2 4.1 copy-start.20
  1039.2 4.0 copy-start.13
  1039.2 4.0 copy-start.19
  1041.3 4.0 copy-start.15
  1051.3 3.1 copy-start.4
  1051.3 3.1 copy-start.16
  1051.3 3.1 copy-start.17
  1051.4 3.1 copy-start.18
  1261.1 2.0 copy-start.23
Sparse Core Ops, SparseCore 0:
  12.2 741.9 all-reduce.2
where the time goes:
time: 1290 us; the launch traced here: 1280 us
  waiting for transfers between devices  855 us (66%)
  blocking collectives  194 us (15%)
  matrix products  79.4 us (6%)
  starting transfers between devices  61 us (5%)
  local copies, waits for them, and re-layouts  57.2 us (4%)
  between operations  20.2 us (2%)
    psum x1, waiting for transfers between devices, spread(): return lax.psum(block, axis)  742 us
    psum x1, blocking collectives, shards(): correlator = lax.psum(partial_sums, 'modes') * norm_scale  194 us
    dot_general x48, matrix products, single(): return jnp.einsum(formula, left_part, right_part, precision=highest)  79.4 us
    all_to_all x4, waiting for transfers between devices, shards(): lax.all_to_all(slab_re, 'modes', split_axis=0, concat_axis=1, tiled=True)  61.6 us
    all_to_all x4, waiting for transfers between devices, shards(): lax.all_to_all(slab_im, 'modes', split_axis=0, concat_axis=1, tiled=True)  51.7 us
    all_to_all x4, starting transfers between devices, shards(): lax.all_to_all(slab_re, 'modes', split_axis=0, concat_axis=1, tiled=True)  35.7 us
  transfers between devices with their start and end apart: 9, of which 7 were waited for; matrix products, arithmetic and copies ran while one was open for 8% of the time, Pallas kernels for 0%

commit v1 on v0

v1 whole, which is shorter than its diff:
```python
import jax
import jax.numpy as jnp
from jax import lax
from jax.experimental import pallas as pl
from jax.experimental.pallas import tpu as pltpu
from jax.sharding import PartitionSpec as P

N = 256
ROWS = 64
MOMS = 2
TIMES = 2
F32 = jnp.float32
BF16 = jnp.bfloat16
VMEM = pl.BlockSpec(memory_space=pltpu.VMEM)
SMEM = pl.BlockSpec(memory_space=pltpu.SMEM)
ANY = pl.BlockSpec(memory_space=pl.ANY)


def halves(x):
    high = x.astype(BF16)
    return high, (x - high.astype(F32)).astype(BF16)


def dot(a, b):
    return jnp.dot(a, b, preferred_element_type=F32)


def dot3(a, b):
    return dot(a[0], b[0]) + (dot(a[0], b[1]) + dot(a[1], b[0]))


def call(body, outs, scratch, limit, flops, nbytes, specs, aliases=None):
    return pl.pallas_call(
        body,
        out_shape=[jax.ShapeDtypeStruct(shape, dtype) for shape, dtype, _ in outs],
        in_specs=specs,
        out_specs=[spec for _, _, spec in outs],
        scratch_shapes=scratch,
        input_output_aliases=aliases or {},
        compiler_params=pltpu.CompilerParams(vmem_limit_bytes=limit << 20),
        cost_estimate=pl.CostEstimate(flops=flops, bytes_accessed=nbytes, transcendentals=0),
    )


def turn_body(elem_ref, high_ref, low_ref):
    for comp in range(2):
        high, low = halves(elem_ref[comp, 0, 0].T)
        high_ref[0, 0, comp * N : (comp + 1) * N, :] = high
        low_ref[0, 0, comp * N : (comp + 1) * N, :] = low


def turn(elementals):
    slab = elementals.shape[2]
    out = jax.ShapeDtypeStruct((MOMS, slab, 2 * N, N), BF16)
    spec = pl.BlockSpec((1, 1, 2 * N, N), lambda m, a: (m, a, 0, 0))
    return pl.pallas_call(
        turn_body,
        grid=(MOMS, slab),
        out_shape=[out, out],
        in_specs=[pl.BlockSpec((2, 1, 1, N, N), lambda m, a: (0, m, a, 0, 0))],
        out_specs=[spec, spec],
        compiler_params=pltpu.CompilerParams(vmem_limit_bytes=16 << 20),
        cost_estimate=pl.CostEstimate(flops=1 << 20, bytes_accessed=8 << 20, transcendentals=0),
    )(elementals)


def first_body(peram_ref, high_ref, low_ref, send_ref, wh_ref, wl_ref):
    for time in range(TIMES):
        re = peram_ref[2 * time]
        im = peram_ref[2 * time + 1]
        for comp, left, right in ((0, re, -im), (1, im, re)):
            rows = pl.ds((2 * time + comp) * ROWS, ROWS)
            for col, part in ((0, left), (N, right)):
                high, low = halves(part)
                wh_ref[rows, col : col + N] = high
                wl_ref[rows, col : col + N] = low

    def step(index, carry):
        mom = index // 4
        a = index % 4
        product = dot3(
            (wh_ref[...], wl_ref[...]), (high_ref[mom, a], low_ref[mom, a])
        )
        for time in range(TIMES):
            for comp in range(2):
                row = (2 * time + comp) * ROWS
                for half in range(2):
                    start = ((mom * TIMES + time) * 2 + half) * 8 + comp * 4 + a
                    send_ref[pl.ds(start, ROWS, stride=64), :] = product[
                        row : row + ROWS, half * 128 : (half + 1) * 128
                    ]
        return carry

    lax.fori_loop(0, 2 * 4, step, 0)


def first(peram, high, low):
    (send,) = call(
        first_body,
        [((ROWS * 64, 128), F32, VMEM)],
        [pltpu.VMEM((4 * ROWS, 2 * N), BF16)] * 2,
        8,
        3 * 2 * 256 * 512 * 256 * 8,
        6 << 20,
        [VMEM] * 3,
    )(peram, high, low)
    return send.reshape(64, 64, 128)


def weights_body(quarter_ref, own_ref, g1_ref, g2_ref, g3_ref, vh_ref, vl_ref, wh_ref, wl_ref):
    quarter = quarter_ref[0]
    nat = lax.broadcasted_iota(jnp.int32, (N, N), 0)
    col = lax.broadcasted_iota(jnp.int32, (N, N), 1)
    place = 4 * (col & 63) + ((quarter + (col >> 6)) & 3)
    order = (nat == place).astype(F32).astype(BF16)
    row = lax.broadcasted_iota(jnp.int32, (2 * N, 2 * N), 0)
    col = lax.broadcasted_iota(jnp.int32, (2 * N, 2 * N), 1)
    place = N * ((col >> 2) & 1) + 4 * (col >> 3) + (col & 3)
    spread = (row == place).astype(F32).astype(BF16)
    for time in range(TIMES):
        parts = []
        for comp in range(2):
            index = 2 * time + comp
            stacked = jnp.concatenate(
                [ref[index] for ref in (own_ref, g1_ref, g2_ref, g3_ref)], axis=0
            )
            parts.append([dot(order, part) for part in halves(stacked)])
        for which, v_ref, w_ref in ((0, vh_ref, wh_ref), (1, vl_ref, wl_ref)):
            re = parts[0][which]
            im = parts[1][which]
            re_t = re.T.astype(BF16)
            im_t = im.T
            v_ref[time, :N, :N] = re_t
            v_ref[time, :N, N:] = im_t.astype(BF16)
            v_ref[time, N:, :N] = (-im_t).astype(BF16)
            v_ref[time, N:, N:] = re_t
            re = re.astype(BF16)
            minus = (-im).astype(BF16)
            im = im.astype(BF16)
            w_ref[time, :N] = (dot(re, spread[:N]) + dot(minus, spread[N:])).astype(BF16)
            w_ref[time, N:] = (dot(im, spread[:N]) + dot(re, spread[N:])).astype(BF16)


def weights(quarter, pieces):
    shape = ((TIMES, 2 * N, 2 * N), BF16, VMEM)
    return call(
        weights_body,
        [shape] * 4,
        [],
        16,
        2 * 2 * 2 * 2 * 256 * 512 * 512,
        5 << 20,
        [SMEM] + [VMEM] * 4,
    )(quarter, *pieces)


def last_body(
    row_ref, pair_ref, got_ref, vh_ref, vl_ref, wh_ref, wl_ref, high_ref, low_ref, sums_ref, old_ref,
    out_ref, total_ref, held, sems,
):
    del old_ref
    row = row_ref[0]
    lane = lax.broadcasted_iota(jnp.int32, (64, 128), 1)

    def copies(index):
        mom, time = index // TIMES, index % TIMES
        return [
            pltpu.make_async_copy(
                held.at[index, comp], out_ref.at[comp, mom, time, row], sems.at[index, comp]
            )
            for comp in range(2)
        ]

    def step(index, totals):
        mom, time = index // TIMES, index % TIMES
        got = jnp.concatenate(
            [
                got_ref[:, pl.ds(pl.multiple_of((index * 2 + half) * 8, 8), 8), :].reshape(512, 128)
                for half in range(2)
            ],
            axis=1,
        )
        first_two = dot3((wh_ref[time], wl_ref[time]), halves(got))
        high, low = halves(first_two)
        full = dot3((high[:N], low[:N]), (vh_ref[time, :N], vl_ref[time, :N])) + dot3(
            (high[N:], low[N:]), (vh_ref[time, N:], vl_ref[time, N:])
        )
        re, im = full[:, :N], full[:, N:]
        held[index, 0] = re.astype(BF16)
        held[index, 1] = im.astype(BF16)
        for copy in copies(index):
            copy.start()
        pair = pair_ref[mom]
        sink = high_ref[pair, row].astype(F32) + low_ref[pair, row].astype(F32)
        sink_re, sink_im = sink[:N], sink[N:]
        real = jnp.sum(sink_re * re + sink_im * im)
        imag = jnp.sum(sink_re * im - sink_im * re)
        totals = totals + jnp.where(lane == index, real, 0.0)
        return totals + jnp.where(lane == index + 4, imag, 0.0)

    total_ref[...] = lax.fori_loop(0, MOMS * TIMES, step, sums_ref[...])
    for index in range(MOMS * TIMES):
        for copy in copies(index):
            copy.wait()


def last(row, pairing, got, tables, high, low, sums, out):
    slab = high.shape[1]
    return call(
        last_body,
        [
            ((2, MOMS, TIMES, slab, N, N), BF16, ANY),
            ((64, 128), F32, VMEM),
        ],
        [pltpu.VMEM((4, 2, N, N), BF16), pltpu.SemaphoreType.DMA((4, 2))],
        16,
        3 * 2 * 2 * 512 * 512 * 256 * 4,
        10 << 20,
        [SMEM, SMEM] + [VMEM] * 8 + [ANY],
        {10: 0},
    )(row, pairing, got, *tables, high, low, sums, out)


def empty_body(out_ref):
    del out_ref


def shards(elementals, perambulators, owners, pairing):
    slab = elementals.shape[2]
    quarter = lax.axis_index("mom").astype(jnp.int32)

    mine = perambulators[0].reshape(TIMES, 2, 64, 4, N)
    mine = lax.dynamic_index_in_dim(mine, quarter, 3, keepdims=False)
    mine = mine.reshape(4, 64, N).transpose(1, 0, 2)
    pieces = lax.all_to_all(mine, "modes", 0, 0, tiled=True)
    piece = jnp.concatenate(
        [
            lax.dynamic_slice(pieces, (owners[time], 2 * time, 0), (1, 2, N))
            for time in range(TIMES)
        ],
        axis=1,
    )
    own = lax.all_to_all(jnp.broadcast_to(piece, (64, 4, N)), "modes", 0, 0, tiled=True)
    own = own.transpose(1, 0, 2)
    quarters = [own] + [
        lax.ppermute(own, "mom", [((i + shift) % 4, i) for i in range(4)]) for shift in (1, 2, 3)
    ]

    high, low = turn(elementals)
    tables = weights(quarter[None], quarters)
    out = pl.pallas_call(
        empty_body,
        out_shape=jax.ShapeDtypeStruct((2, MOMS, TIMES, slab, N, N), BF16),
        out_specs=ANY,
    )()
    sums = jnp.zeros((64, 128), F32)
    for shift in range(4):
        sent = first(quarters[shift], high, low)
        got = lax.all_to_all(sent, "modes", 0, 0, tiled=True)
        row = (quarter + shift) % 4
        out, sums = last(row[None], pairing, got, tables, high, low, sums, out)
    sums = lax.all_to_all(sums, "modes", 0, 0, tiled=True)
    correlator = jnp.sum(sums[:, :8], axis=0).reshape(2, MOMS, TIMES) * float(N) ** -1.5
    return out, correlator


def solution(mesh):
    placed = (
        P(None, "mom", "modes", None, None),
        P("modes", None, None, None, None),
        P(),
        P("mom"),
    )
    return jax.shard_map(
        shards,
        mesh=mesh,
        in_specs=placed,
        out_specs=(P(None, "mom", None, "modes", None, None), P(None, "mom", None)),
        check_vma=False,
    )
```

time: 1290 us -> 359 us (0.28)
  waiting for transfers between devices: 855 us -> 183 us
  blocking collectives: 194 us -> 17.4 us
  matrix products: 79.4 us -> 0 us
  Pallas kernels: 0 us -> 60.6 us
  local copies, waits for them, and re-layouts: 57.2 us -> 30.4 us
  between operations: 20.2 us -> 4.58 us
    psum x1 -> x0, waiting for transfers between devices: 742 us -> none  [spread(): return lax.psum(block, axis)]
    psum x1 -> x0, blocking collectives: 194 us -> none  [shards(): correlator = lax.psum(partial_sums, 'modes') * norm_scale]
    ppermute x0 -> x3, waiting for transfers between devices: none -> 146 us  [shards(): lax.ppermute(own, 'mom', [((i + shift) % 4, i) for i in range(4)])]
    dot_general x48 -> x0, matrix products: 79.4 us -> none  [single(): return jnp.einsum(formula, left_part, right_part, precision=highest)]
    all_to_all x8 -> x6, waiting for transfers between devices: 113 us -> 36.9 us  [the longest x4 17 us: shards(): got = lax.all_to_all(sent, 'modes', 0, 0, tiled=True)]
    pallas_call x0 -> x11, Pallas kernels: none -> 60.6 us  [the longest x4 40.3 us: last(): call(last_body, [((2, MOMS, TIMES, slab, N, N), BF16, ANY), ((64, 128), F...]
    all_to_all x16 -> x1, local copies, waits for them, and re-layouts: 34.7 us -> 0.05 us  [shards(): lax.all_to_all(jnp.broadcast_to(piece, (64, 4, N)), 'modes', 0, 0, tiled=...]
    unnamed x51 -> x53, local copies, waits for them, and re-layouts: 7.34 us -> 25.6 us
  transfers between devices with their start and end apart: 9 -> 9, of which waited for: 7 -> 6; matrix products, arithmetic and copies ran while one was open for 8% -> 0% of each run, Pallas kernels for 0% -> 13%
where the time goes in v1:
time: 359 us; the launch traced here: 357 us
  waiting for transfers between devices  183 us (51%)
  starting transfers between devices  61.7 us (17%)
  Pallas kernels  60.6 us (17%)
  local copies, waits for them, and re-layouts  30.4 us (8%)
  blocking collectives  17.4 us (5%)
  between operations  4.58 us (1%)
    ppermute x3, waiting for transfers between devices, shards(): lax.ppermute(own, 'mom', [((i + shift) % 4, i) for i in range(4)])  146 us
    all_to_all x4, starting transfers between devices, shards(): got = lax.all_to_all(sent, 'modes', 0, 0, tiled=True)  41.9 us
    pallas_call x4, Pallas kernels, last(): call(last_body, [((2, MOMS, TIMES, slab, N, N), BF16, ANY), ((64, 128), F...  40.3 us
    unnamed x53, local copies, waits for them, and re-layouts  25.6 us
    all_to_all x1, blocking collectives, shards(): sums = lax.all_to_all(sums, 'modes', 0, 0, tiled=True)  17.4 us
    all_to_all x4, waiting for transfers between devices, shards(): got = lax.all_to_all(sent, 'modes', 0, 0, tiled=True)  17 us
    pallas_call x4, Pallas kernels, first(): call(first_body, [((ROWS * 64, 128), F32, VMEM)], [pltpu.VMEM((4 * ROWS,...  16.6 us
    all_to_all x1, starting transfers between devices, shards(): pieces = lax.all_to_all(mine, 'modes', 0, 0, tiled=True)  13.7 us
  transfers between devices with their start and end apart: 9, of which 6 were waited for; matrix products, arithmetic and copies ran while one was open for 0% of the time, Pallas kernels for 13%

profile of v1, /device:TPU:32, one launch (start us, length us, event | category | flops | bytes accessed | tf_op | source)
XLA Modules:
  0.0 357.3 jit_solution(12023934667100852185)
XLA Ops:
  0.6 1.5 reshape_squeeze.3
  2.5 0.9 copy.18
  3.4 13.7 %all-to-all-start = ((f32[64,4,256]{2,1,0:T(4,128)}), f32[64,4,256]{2,1,0:T(4,128)S(1)}, u32[]{:S(2)}, u32[]{:S(2)}) async-start(f32[64,4,256]{2,1,0:T(4,128)} %bitcast.24), calls=%async_computation | async-start | bytes 524288 | tf_op jit(solution)/shard_map/all_to_all | solution.py:235
  21.2 11.2 %all-to-all-done = f32[64,4,256]{2,1,0:T(4,128)S(1)} async-done(((f32[64,4,256]{2,1,0:T(4,128)}), f32[64,4,256]{2,1,0:T(4,128)S(1)}, u32[]{:S(2)}, u32[]{:S(2)}) %all-to-all-start) | async-done | bytes 262176 | tf_op jit(solution)/shard_map/all_to_all | solution.py:235
  32.4 0.7 broadcast_in_dim.27
  33.2 4.6 %all-to-all-start.1 = ((f32[64,4,256]{2,1,0:T(4,128)}), f32[64,4,256]{2,1,0:T(4,128)S(1)}, u32[]{:S(2)}, u32[]{:S(2)}) async-start(f32[64,4,256]{2,1,0:T(4,128)} %broadcast_in_dim.27), calls=%async_computation.1 | async-start | bytes 524288 | tf_op jit(solution)/shard_map/all_to_all | solution.py:243
  37.8 2.2 copy-done.17
  40.0 2.1 shard_map.59
  42.1 1.3 copy-done
  43.4 8.7 %all-to-all-done.1 = f32[64,4,256]{2,1,0:T(4,128)S(1)} async-done(((f32[64,4,256]{2,1,0:T(4,128)}), f32[64,4,256]{2,1,0:T(4,128)S(1)}, u32[]{:S(2)}, u32[]{:S(2)}) %all-to-all-start.1) | async-done | bytes 262176 | tf_op jit(solution)/shard_map/all_to_all | solution.py:243
  52.2 1.6 copy-done.1
  53.7 4.1 %shard_map.64 = f32[4096,128]{1,0:T(8,128)S(1)} custom-call(f32[4,64,256]{2,1,0:T(8,128)S(1)} %bitcast.30, bf16[2,4,512,256]{3,2,1,0:T(8,128)(2,1)S(1)} %get-tuple-element.16.high_ref, bf16[2,4,512,256]{3,2,1,0:T(8,128)(2,1)S(1)} %copy-done.1), custom_call_target="tpu_custom_call" | custom-call | flops 1610612736 | bytes 6291456 | tf_op jit(solution)/shard_map/pallas_call | solution.py:98
  57.9 1.3 copy-done.16
  59.2 5.6 %all-to-all-start.5 = ((f32[64,64,128]{2,1,0:T(8,128)}), f32[64,64,128]{2,1,0:T(8,128)}, u32[]{:S(2)}, u32[]{:S(2)}) async-start(f32[64,64,128]{2,1,0:T(8,128)} %bitcast.29), calls=%async_computation.5 | async-start | bytes 4194304 | tf_op jit(solution)/shard_map/all_to_all | solution.py:259
  64.9 44.8 %collective-permute-done.1.g1_ref.peram_ref = f32[4,64,256]{2,1,0:T(8,128)S(1)} collective-permute-done((f32[4,64,256]{2,1,0:T(8,128)S(1)}, f32[4,64,256]{2,1,0:T(8,128)S(1)}, u32[]{:S(2)}, u32[]{:S(2)}) %collective-permute-start.1) | collective-permute-done | bytes 262176 | tf_op jit(solution)/shard_map/ppermute | solution.py:246
  109.7 1.6 copy-done.2
  111.3 4.1 %shard_map.63 = f32[4096,128]{1,0:T(8,128)S(1)} custom-call(f32[4,64,256]{2,1,0:T(8,128)S(1)} %collective-permute-done.1.g1_ref.peram_ref, bf16[2,4,512,256]{3,2,1,0:T(8,128)(2,1)S(1)} %get-tuple-element.16.high_ref, bf16[2,4,512,256]{3,2,1,0:T(8,128)(2,1)S(1)} %copy-done.2), custom_call_target="tpu_custom_call" | custom-call | flops 1610612736 | bytes 6291456 | tf_op jit(solution)/shard_map/pallas_call | solution.py:98
  115.4 1.3 copy-done.14
  116.8 0.7 copy-done.18
  117.5 12.1 %all-to-all-start.4 = ((f32[64,64,128]{2,1,0:T(8,128)}), f32[64,64,128]{2,1,0:T(8,128)}, u32[]{:S(2)}, u32[]{:S(2)}) async-start(f32[64,64,128]{2,1,0:T(8,128)} %bitcast.27), calls=%async_computation.4 | async-start | bytes 4194304 | tf_op jit(solution)/shard_map/all_to_all | solution.py:259
  129.6 1.4 collective-permute-start.2
  131.0 51.9 %collective-permute-done.2.g2_ref.peram_ref = f32[4,64,256]{2,1,0:T(8,128)S(1)} collective-permute-done((f32[4,64,256]{2,1,0:T(8,128)S(1)}, f32[4,64,256]{2,1,0:T(8,128)S(1)}, u32[]{:S(2)}, u32[]{:S(2)}) %collective-permute-start.2) | collective-permute-done | bytes 262176 | tf_op jit(solution)/shard_map/ppermute | solution.py:246
  182.9 1.6 copy-done.3
  184.5 4.1 %shard_map.62 = f32[4096,128]{1,0:T(8,128)S(1)} custom-call(f32[4,64,256]{2,1,0:T(8,128)S(1)} %collective-permute-done.2.g2_ref.peram_ref, bf16[2,4,512,256]{3,2,1,0:T(8,128)(2,1)S(1)} %get-tuple-element.16.high_ref, bf16[2,4,512,256]{3,2,1,0:T(8,128)(2,1)S(1)} %copy-done.3), custom_call_target="tpu_custom_call" | custom-call | flops 1610612736 | bytes 6291456 | tf_op jit(solution)/shard_map/pallas_call | solution.py:98
  188.6 1.3 copy-done.15
  189.9 0.7 copy-done.20
  190.7 12.0 %all-to-all-start.3 = ((f32[64,64,128]{2,1,0:T(8,128)}), f32[64,64,128]{2,1,0:T(8,128)}, u32[]{:S(2)}, u32[]{:S(2)}) async-start(f32[64,64,128]{2,1,0:T(8,128)} %bitcast.28), calls=%async_computation.3 | async-start | bytes 4194304 | tf_op jit(solution)/shard_map/all_to_all | solution.py:259
  202.7 48.9 %collective-permute-done.peram_ref.g3_ref = f32[4,64,256]{2,1,0:T(8,128)S(1)} collective-permute-done((f32[4,64,256]{2,1,0:T(8,128)S(1)}, f32[4,64,256]{2,1,0:T(8,128)S(1)}, u32[]{:S(2)}, u32[]{:S(2)}) %collective-permute-start) | collective-permute-done | bytes 262176 | tf_op jit(solution)/shard_map/ppermute | solution.py:246
  251.7 1.6 copy-done.4
  253.2 4.1 %shard_map.60 = f32[4096,128]{1,0:T(8,128)S(1)} custom-call(f32[4,64,256]{2,1,0:T(8,128)S(1)} %collective-permute-done.peram_ref.g3_ref, bf16[2,4,512,256]{3,2,1,0:T(8,128)(2,1)S(1)} %get-tuple-element.16.high_ref, bf16[2,4,512,256]{3,2,1,0:T(8,128)(2,1)S(1)} %copy-done.4), custom_call_target="tpu_custom_call" | custom-call | flops 1610612736 | bytes 6291456 | tf_op jit(solution)/shard_map/pallas_call | solution.py:98
  257.4 1.3 copy-done.13
  258.7 0.7 copy-done.22
  259.4 12.3 %all-to-all-start.2 = ((f32[64,64,128]{2,1,0:T(8,128)}), f32[64,64,128]{2,1,0:T(8,128)}, u32[]{:S(2)}, u32[]{:S(2)}) async-start(f32[64,64,128]{2,1,0:T(8,128)} %bitcast.26), calls=%async_computation.2 | async-start | bytes 4194304 | tf_op jit(solution)/shard_map/all_to_all | solution.py:259
  271.8 1.1 copy-done.19
  272.9 0.9 copy-done.21
  273.8 0.9 copy-done.23
  274.8 1.7 shard_map.61
  276.6 10.9 %shard_map.66 = (bf16[2,2,2,4,256,256]{5,4,3,2,1,0:T(8,128)(2,1)}, f32[64,128]{1,0:T(8,128)S(1)}) custom-call(s32[1]{0:T(128)} %bitcast.12.row_ref, s32[2]{0:T(128)S(1)} %copy-done.24, f32[64,64,128]{2,1,0:T(8,128)} %all-to-all-done.5.got_ref, bf16[2,512,512]{2,1,0:T(8,128)(2,1)S(1)} %get-tuple-element.18.vh_ref, ...), custom_call_target="tpu_custom_call", output_to_operand_aliasing={{0}: (10, {})} | custom-call | flops 3221225472 | bytes 10485760 | tf_op jit(solution)/shard_map/pallas_call | solution.py:209
  287.4 9.8 %shard_map.67 = (bf16[2,2,2,4,256,256]{5,4,3,2,1,0:T(8,128)(2,1)}, f32[64,128]{1,0:T(8,128)S(1)}) custom-call(s32[1]{0:T(128)} %bitcast.10.row_ref, s32[2]{0:T(128)S(1)} %copy-done.24, f32[64,64,128]{2,1,0:T(8,128)} %all-to-all-done.4.got_ref, bf16[2,512,512]{2,1,0:T(8,128)(2,1)S(1)} %get-tuple-element.18.vh_ref, ...), custom_call_target="tpu_custom_call", output_to_operand_aliasing={{0}: (10, {})} | custom-call | flops 3221225472 | bytes 10485760 | tf_op jit(solution)/shard_map/pallas_call | solution.py:209
  297.3 9.8 %shard_map.68 = (bf16[2,2,2,4,256,256]{5,4,3,2,1,0:T(8,128)(2,1)}, f32[64,128]{1,0:T(8,128)S(1)}) custom-call(s32[1]{0:T(128)} %bitcast.8.row_ref, s32[2]{0:T(128)S(1)} %copy-done.24, f32[64,64,128]{2,1,0:T(8,128)} %all-to-all-done.3.got_ref, bf16[2,512,512]{2,1,0:T(8,128)(2,1)S(1)} %get-tuple-element.18.vh_ref, ...), custom_call_target="tpu_custom_call", output_to_operand_aliasing={{0}: (10, {})} | custom-call | flops 3221225472 | bytes 10485760 | tf_op jit(solution)/shard_map/pallas_call | solution.py:209
  307.1 17.0 %all-to-all-done.2.got_ref = f32[64,64,128]{2,1,0:T(8,128)} async-done(((f32[64,64,128]{2,1,0:T(8,128)}), f32[64,64,128]{2,1,0:T(8,128)}, u32[]{:S(2)}, u32[]{:S(2)}) %all-to-all-start.2) | async-done | bytes 2097184 | tf_op jit(solution)/shard_map/all_to_all | solution.py:259
  324.1 1.6 copy-done.6
  325.7 1.2 copy-done.8
  326.9 1.2 copy-done.10
  328.2 1.2 copy-done.12
  329.4 9.8 %shard_map.69 = (bf16[2,2,2,4,256,256]{5,4,3,2,1,0:T(8,128)(2,1)}, f32[64,128]{1,0:T(8,128)S(1)}) custom-call(s32[1]{0:T(128)} %bitcast.row_ref, s32[2]{0:T(128)S(1)} %copy-done.24, f32[64,64,128]{2,1,0:T(8,128)} %all-to-all-done.2.got_ref, bf16[2,512,512]{2,1,0:T(8,128)(2,1)S(1)} %get-tuple-element.18.vh_ref, ...), custom_call_target="tpu_custom_call", output_to_operand_aliasing={{0}: (10, {})} | custom-call | flops 3221225472 | bytes 10485760 | tf_op jit(solution)/shard_map/pallas_call | solution.py:209
  339.2 17.4 %all_to_all.42 = f32[64,1,128]{2,1,0:T(1,128)S(1)} all-to-all(f32[64,1,128]{2,1,0:T(1,128)S(1)} %bitcast.35), channel_id=1, replica_groups=mesh['modes'=64,'mom'=4] {'modes'}, dimensions={0} | all-to-all | bytes 65536 | tf_op jit(solution)/shard_map/all_to_all | solution.py:262
  356.6 0.7 mul.7
  (47 shorter events, 1.3 us)
Async XLA Ops:
  0.6 16.4 %copy-start.25 = (s32[2]{0:T(128)S(1)}, s32[2]{0:T(128)}, u32[]{:S(2)}) copy-start(s32[2]{0:T(128)} %param.6) | copy-start | bytes 28
  3.4 29.0 %all-to-all-start = ((f32[64,4,256]{2,1,0:T(4,128)}), f32[64,4,256]{2,1,0:T(4,128)S(1)}, u32[]{:S(2)}, u32[]{:S(2)}) async-start(f32[64,4,256]{2,1,0:T(4,128)} %bitcast.24), calls=%async_computation | async-start | bytes 524288 | tf_op jit(solution)/shard_map/all_to_all | solution.py:235
  33.2 18.9 %all-to-all-start.1 = ((f32[64,4,256]{2,1,0:T(4,128)}), f32[64,4,256]{2,1,0:T(4,128)S(1)}, u32[]{:S(2)}, u32[]{:S(2)}) async-start(f32[64,4,256]{2,1,0:T(4,128)} %broadcast_in_dim.27), calls=%async_computation.1 | async-start | bytes 524288 | tf_op jit(solution)/shard_map/all_to_all | solution.py:243
  37.8 2.2 copy-start.17
  42.1 1.3 copy-start
  52.2 1.6 copy-start.1
  57.9 1.3 copy-start.16
  59.2 58.3 %all-to-all-start.5 = ((f32[64,64,128]{2,1,0:T(8,128)}), f32[64,64,128]{2,1,0:T(8,128)}, u32[]{:S(2)}, u32[]{:S(2)}) async-start(f32[64,64,128]{2,1,0:T(8,128)} %bitcast.29), calls=%async_computation.5 | async-start | bytes 4194304 | tf_op jit(solution)/shard_map/all_to_all | solution.py:259
  64.8 44.9 %collective-permute-start.1 = (f32[4,64,256]{2,1,0:T(8,128)S(1)}, f32[4,64,256]{2,1,0:T(8,128)S(1)}, u32[]{:S(2)}, u32[]{:S(2)}) collective-permute-start(f32[4,64,256]{2,1,0:T(8,128)S(1)} %bitcast.31), channel_id=1, source_target_pairs={{1,0},{2,1},{3,2},{0,3},{5,4},{6,5},{7,6},{4,7},{9,8},{10,9},{11,1... | collective-permute-start | bytes 786440 | tf_op jit(solution)/shard_map/ppermute | solution.py:246
  109.7 1.6 copy-start.2
  115.4 1.3 copy-start.14
  116.8 0.7 copy-start.18
  117.5 73.2 %all-to-all-start.4 = ((f32[64,64,128]{2,1,0:T(8,128)}), f32[64,64,128]{2,1,0:T(8,128)}, u32[]{:S(2)}, u32[]{:S(2)}) async-start(f32[64,64,128]{2,1,0:T(8,128)} %bitcast.27), calls=%async_computation.4 | async-start | bytes 4194304 | tf_op jit(solution)/shard_map/all_to_all | solution.py:259
  129.6 53.3 %collective-permute-start.2 = (f32[4,64,256]{2,1,0:T(8,128)S(1)}, f32[4,64,256]{2,1,0:T(8,128)S(1)}, u32[]{:S(2)}, u32[]{:S(2)}) collective-permute-start(f32[4,64,256]{2,1,0:T(8,128)S(1)} %bitcast.32), channel_id=1, source_target_pairs={{2,0},{3,1},{0,2},{1,3},{6,4},{7,5},{4,6},{5,7},{10,8},{11,9},{8,1... | collective-permute-start | bytes 786440 | tf_op jit(solution)/shard_map/ppermute | solution.py:246
  182.9 1.6 copy-start.3
  188.6 1.3 copy-start.15
  189.9 0.7 copy-start.20
  190.7 68.8 %all-to-all-start.3 = ((f32[64,64,128]{2,1,0:T(8,128)}), f32[64,64,128]{2,1,0:T(8,128)}, u32[]{:S(2)}, u32[]{:S(2)}) async-start(f32[64,64,128]{2,1,0:T(8,128)} %bitcast.28), calls=%async_computation.3 | async-start | bytes 4194304 | tf_op jit(solution)/shard_map/all_to_all | solution.py:259
  202.6 49.0 %collective-permute-start = (f32[4,64,256]{2,1,0:T(8,128)S(1)}, f32[4,64,256]{2,1,0:T(8,128)S(1)}, u32[]{:S(2)}, u32[]{:S(2)}) collective-permute-start(f32[4,64,256]{2,1,0:T(8,128)S(1)} %bitcast.33), channel_id=1, source_target_pairs={{3,0},{0,1},{1,2},{2,3},{7,4},{4,5},{5,6},{6,7},{11,8},{8,9},{9,10... | collective-permute-start | bytes 786440 | tf_op jit(solution)/shard_map/ppermute | solution.py:246
  251.7 1.6 copy-start.4
  257.4 1.3 copy-start.13
  258.7 0.7 copy-start.22
  259.4 64.7 %all-to-all-start.2 = ((f32[64,64,128]{2,1,0:T(8,128)}), f32[64,64,128]{2,1,0:T(8,128)}, u32[]{:S(2)}, u32[]{:S(2)}) async-start(f32[64,64,128]{2,1,0:T(8,128)} %bitcast.26), calls=%async_computation.2 | async-start | bytes 4194304 | tf_op jit(solution)/shard_map/all_to_all | solution.py:259
  271.7 4.8 %copy-start.24 = (s32[2]{0:T(128)S(1)}, s32[2]{0:T(128)}, u32[]{:S(2)}) copy-start(s32[2]{0:T(128)} %pair_ref.7) | copy-start | bytes 28
  271.8 4.8 %copy-start.5 = (bf16[2,4,512,256]{3,2,1,0:T(8,128)(2,1)S(1)}, bf16[2,4,512,256]{3,2,1,0:T(8,128)(2,1)}, u32[]{:S(2)}) copy-start(bf16[2,4,512,256]{3,2,1,0:T(8,128)(2,1)} %copy-done) | copy-start | bytes 6291460
  271.8 1.1 copy-start.19
  272.9 0.9 copy-start.21
  273.8 0.9 copy-start.23
  276.5 20.8 %copy-start.7 = (bf16[2,512,512]{2,1,0:T(8,128)(2,1)}, bf16[2,512,512]{2,1,0:T(8,128)(2,1)S(1)}, u32[]{:S(2)}) copy-start(bf16[2,512,512]{2,1,0:T(8,128)(2,1)S(1)} %get-tuple-element.19.vl_ref) | copy-start | bytes 3145732
  276.5 20.8 %copy-start.9 = (bf16[2,512,512]{2,1,0:T(8,128)(2,1)}, bf16[2,512,512]{2,1,0:T(8,128)(2,1)S(1)}, u32[]{:S(2)}) copy-start(bf16[2,512,512]{2,1,0:T(8,128)(2,1)S(1)} %get-tuple-element.20.wh_ref) | copy-start | bytes 3145732
  276.5 20.8 %copy-start.11 = (bf16[2,512,512]{2,1,0:T(8,128)(2,1)}, bf16[2,512,512]{2,1,0:T(8,128)(2,1)S(1)}, u32[]{:S(2)}) copy-start(bf16[2,512,512]{2,1,0:T(8,128)(2,1)S(1)} %get-tuple-element.21.wl_ref) | copy-start | bytes 3145732
  324.1 1.6 copy-start.6
  325.7 1.2 copy-start.8
  326.9 1.2 copy-start.10
  328.2 1.2 copy-start.12

commit v2 on v1

v2 whole, which is shorter than its diff:
```python
import functools

import jax
import jax.numpy as jnp
from jax import lax
from jax.experimental import pallas as pl
from jax.experimental.pallas import tpu as pltpu
from jax.sharding import PartitionSpec as P

N = 256
ROWS = 64
MOMS = 2
TIMES = 2
F32 = jnp.float32
BF16 = jnp.bfloat16
VMEM = pl.BlockSpec(memory_space=pltpu.VMEM)
SMEM = pl.BlockSpec(memory_space=pltpu.SMEM)
ANY = pl.BlockSpec(memory_space=pl.ANY)


def halves(x):
    high = x.astype(BF16)
    return high, (x - high.astype(F32)).astype(BF16)


def dot(a, b):
    return jnp.dot(a, b, preferred_element_type=F32)


def dot3(a, b):
    left = jnp.concatenate([a[0], a[0], a[1]], axis=1)
    return dot(left, jnp.concatenate([b[0], b[1], b[0]], axis=0))


def params(flops, nbytes):
    return dict(
        cost_estimate=pl.CostEstimate(flops=flops, bytes_accessed=nbytes, transcendentals=0),
    )


def turn_body(elem_ref, high_ref, low_ref):
    for comp in range(2):
        high, low = halves(elem_ref[comp, 0, 0].T)
        high_ref[0, 0, comp * N : (comp + 1) * N, :] = high
        low_ref[0, 0, comp * N : (comp + 1) * N, :] = low


def turn(elementals):
    slab = elementals.shape[2]
    out = jax.ShapeDtypeStruct((MOMS, slab, 2 * N, N), BF16)
    spec = pl.BlockSpec((1, 1, 2 * N, N), lambda m, a: (m, a, 0, 0))
    return pl.pallas_call(
        turn_body,
        grid=(MOMS, slab),
        out_shape=[out, out],
        in_specs=[pl.BlockSpec((2, 1, 1, N, N), lambda m, a: (0, m, a, 0, 0))],
        out_specs=[spec, spec],
        **params(1 << 20, 8 << 20),
    )(elementals)


def first_body(count, *refs):
    perams, (high_hbm, low_hbm, send_hbm), refs = refs[:count], refs[count : count + 3], refs[count + 3 :]
    wh_ref, wl_ref, high_ref, low_ref, send_ref, in_sems, out_sems = refs
    slab = high_ref.shape[1]

    def loads(mom, a):
        return [
            pltpu.make_async_copy(src.at[mom, a], dst.at[mom, a], in_sems.at[which, mom, a])
            for which, (src, dst) in enumerate(((high_hbm, high_ref), (low_hbm, low_ref)))
        ]

    def store(mom):
        rows = pl.ds(mom * count * 32, count * 32)
        return pltpu.make_async_copy(send_ref.at[mom], send_hbm.at[:, rows, :], out_sems.at[mom])

    for mom in range(MOMS):
        for a in range(slab):
            for copy in loads(mom, a):
                copy.start()
    for index, ref in enumerate(perams):
        for time in range(TIMES):
            re = ref[2 * time]
            im = ref[2 * time + 1]
            for comp, left, right in ((0, re, -im), (1, im, re)):
                row = ((index * TIMES + time) * 2 + comp) * ROWS
                for col, part in ((0, left), (N, right)):
                    high, low = halves(part)
                    wh_ref[row : row + ROWS, col : col + N] = high
                    wl_ref[row : row + ROWS, col : col + N] = low

    for mom in range(MOMS):
        flat = send_ref.at[mom].reshape(64 * count * 32, 128)

        def step(a, carry, mom=mom, flat=flat):
            for copy in loads(mom, a):
                copy.wait()
            elem = (high_ref[mom, a], low_ref[mom, a])
            for index in range(count):
                rows = slice(index * 4 * ROWS, (index + 1) * 4 * ROWS)
                product = dot3((wh_ref[rows], wl_ref[rows]), elem)
                for time in range(TIMES):
                    for comp in range(2):
                        row = (2 * time + comp) * ROWS
                        for half in range(2):
                            start = ((index * TIMES + time) * 2 + half) * 8 + comp * 4 + a
                            flat[pl.ds(start, ROWS, stride=count * 32), :] = product[
                                row : row + ROWS, half * 128 : (half + 1) * 128
                            ]
            return carry

        lax.fori_loop(0, slab, step, 0)
        store(mom).start()
    for mom in range(MOMS):
        store(mom).wait()


def first(perams, high, low):
    count, slab = len(perams), high.shape[1]
    return pl.pallas_call(
        functools.partial(first_body, count),
        in_specs=[VMEM] * count + [ANY, ANY],
        out_specs=ANY,
        out_shape=jax.ShapeDtypeStruct((64, MOMS * count * 32, 128), F32),
        scratch_shapes=[pltpu.VMEM((count * 4 * ROWS, 2 * N), BF16)] * 2
        + [pltpu.VMEM((MOMS, slab, 2 * N, N), BF16)] * 2
        + [
            pltpu.VMEM((MOMS, 64, count * 32, 128), F32),
            pltpu.SemaphoreType.DMA((2, MOMS, slab)),
            pltpu.SemaphoreType.DMA((MOMS,)),
        ],
        **params(count * 3 * 2 * 256 * 512 * 256 * 8, 6 << 20),
    )(*perams, high, low)


def weights_body(quarter_ref, own_ref, g1_ref, g2_ref, g3_ref, vh_ref, vl_ref, wh_ref, wl_ref):
    quarter = quarter_ref[0]
    nat = lax.broadcasted_iota(jnp.int32, (N, N), 0)
    col = lax.broadcasted_iota(jnp.int32, (N, N), 1)
    place = 4 * (col & 63) + (quarter ^ (col >> 6))
    order = (nat == place).astype(F32).astype(BF16)
    row = lax.broadcasted_iota(jnp.int32, (2 * N, 2 * N), 0)
    col = lax.broadcasted_iota(jnp.int32, (2 * N, 2 * N), 1)
    place = N * ((col >> 2) & 1) + 4 * (col >> 3) + (col & 3)
    spread = (row == place).astype(F32).astype(BF16)
    for time in range(TIMES):
        parts = []
        for comp in range(2):
            index = 2 * time + comp
            stacked = jnp.concatenate(
                [ref[index] for ref in (own_ref, g1_ref, g2_ref, g3_ref)], axis=0
            )
            parts.append([dot(order, part) for part in halves(stacked)])
        for which, v_ref, w_ref in ((0, vh_ref, wh_ref), (1, vl_ref, wl_ref)):
            re = parts[0][which]
            im = parts[1][which]
            re_t = re.T.astype(BF16)
            im_t = im.T
            v_ref[time, :N, :N] = re_t
            v_ref[time, :N, N:] = im_t.astype(BF16)
            v_ref[time, N:, :N] = (-im_t).astype(BF16)
            v_ref[time, N:, N:] = re_t
            re = re.astype(BF16)
            minus = (-im).astype(BF16)
            im = im.astype(BF16)
            w_ref[time, :N] = (dot(re, spread[:N]) + dot(minus, spread[N:])).astype(BF16)
            w_ref[time, N:] = (dot(im, spread[:N]) + dot(re, spread[N:])).astype(BF16)


def weights(quarter, pieces):
    return pl.pallas_call(
        weights_body,
        in_specs=[SMEM] + [VMEM] * 4,
        out_specs=[VMEM] * 4,
        out_shape=[jax.ShapeDtypeStruct((TIMES, 2 * N, 2 * N), BF16)] * 4,
        **params(2 * 2 * 2 * 2 * 256 * 512 * 512, 5 << 20),
    )(quarter, *pieces)


def add_sums(sums_ref, total_ref, index, start, real, imag):
    @pl.when(start)
    def _():
        total_ref[...] = sums_ref[...]

    lane = lax.broadcasted_iota(jnp.int32, (64, 128), 1)
    total_ref[...] += jnp.where(lane == index, real, 0.0) + jnp.where(lane == index + 4, imag, 0.0)


def last_body(row_ref, pair_ref, got_ref, vh_ref, vl_ref, wh_ref, wl_ref, *refs):
    del row_ref, pair_ref
    out_ref = refs[-1] if len(refs) == 2 else refs[-2]
    got = jnp.concatenate(
        [got_ref[:, half * 8 : (half + 1) * 8, :].reshape(512, 128) for half in range(2)], axis=1
    )
    second = dot3((wh_ref[0], wl_ref[0]), halves(got))
    high, low = [jnp.concatenate([part[:N], part[N:]], axis=1) for part in halves(second)]
    full = dot3((high, low), (vh_ref[0], vl_ref[0]))
    re, im = full[:, :N], full[:, N:]
    out_ref[0, 0, 0, 0] = re.astype(BF16)
    out_ref[1, 0, 0, 0] = im.astype(BF16)
    if len(refs) == 2:
        return
    high_ref, low_ref, sums_ref, _, _, total_ref = refs
    sink = high_ref[0, 0].astype(F32) + low_ref[0, 0].astype(F32)
    sink_re, sink_im = sink[:N], sink[N:]
    real = jnp.sum(sink_re * re + sink_im * im)
    imag = jnp.sum(sink_re * im - sink_im * re)
    time, mom = pl.program_id(0), pl.program_id(1)
    add_sums(sums_ref, total_ref, mom * TIMES + time, (time == 0) & (mom == 0), real, imag)


TABLE = pl.BlockSpec((1, 2 * N, 2 * N), lambda t, m, row, pair: (t, 0, 0))
ELEM = pl.BlockSpec((1, 1, 2 * N, N), lambda t, m, row, pair: (pair[m], row[0], 0, 0))


def last(row, pairing, got, count, which, tables, high, low, sums, out):
    whole = pl.BlockSpec((64, 128), lambda t, m, row, pair: (0, 0))
    block = pl.BlockSpec(
        (64, 16, 128), lambda t, m, row, pair: (0, (m * count + which) * TIMES + t, 0)
    )
    with_sums = sums is not None
    result = pl.pallas_call(
        last_body,
        grid_spec=pltpu.PrefetchScalarGridSpec(
            num_scalar_prefetch=2,
            grid=(TIMES, MOMS),
            in_specs=[block] + [TABLE] * 4 + ([ELEM, ELEM, whole] if with_sums else []) + [ANY],
            out_specs=[
                pl.BlockSpec((2, 1, 1, 1, N, N), lambda t, m, row, pair: (0, m, t, row[0], 0, 0))
            ]
            + ([whole] if with_sums else []),
        ),
        out_shape=[jax.ShapeDtypeStruct(out.shape, BF16)]
        + ([jax.ShapeDtypeStruct((64, 128), F32)] if with_sums else []),
        input_output_aliases={10 if with_sums else 7: 0},
        **params(3 * 2 * 2 * 512 * 512 * 256 * 4, 10 << 20),
    )(row, pairing, got, *tables, *((high, low, sums) if with_sums else ()), out)
    return result if with_sums else (result[0], None)


def dual_body(row_ref, pair_ref, vh_ref, vl_ref, wh_ref, wl_ref, high_ref, low_ref, out_ref):
    del row_ref, pair_ref
    high, low = [
        jnp.concatenate([ref[0, 0, :N], ref[0, 0, N:]], axis=1) for ref in (high_ref, low_ref)
    ]
    second = lax.dot_general(
        jnp.concatenate([high, high, low], axis=1),
        jnp.concatenate([vh_ref[0], vl_ref[0], vh_ref[0]], axis=1),
        (((1,), (1,)), ((), ())),
        preferred_element_type=F32,
    )
    high, low = halves(jnp.concatenate([second[:, :N], second[:, N:]], axis=0))
    full = lax.dot_general(
        jnp.concatenate([wh_ref[0], wh_ref[0], wl_ref[0]], axis=0),
        jnp.concatenate([high, low, high], axis=0),
        (((0,), (0,)), ((), ())),
        preferred_element_type=F32,
    )
    for half in range(2):
        out_ref[:, half * 8 : (half + 1) * 8, :] = full[:, half * 128 : (half + 1) * 128].reshape(
            64, 8, 128
        )


def dual(row, pairing, tables, high, low):
    return pl.pallas_call(
        dual_body,
        grid_spec=pltpu.PrefetchScalarGridSpec(
            num_scalar_prefetch=2,
            grid=(TIMES, MOMS),
            in_specs=[TABLE] * 4 + [ELEM, ELEM],
            out_specs=pl.BlockSpec((64, 16, 128), lambda t, m, row, pair: (0, m * TIMES + t, 0)),
        ),
        out_shape=jax.ShapeDtypeStruct((64, 64, 128), F32),
        **params(3 * 2 * 2 * 512 * 512 * 256 * 4, 8 << 20),
    )(row, pairing, *tables, high, low)


def meet_body(got_ref, dual_hbm, sums_hbm, total_ref, dual_ref, sums_ref, sems):
    copies = [
        pltpu.make_async_copy(
            dual_hbm.at[:, index * 16 : (index + 1) * 16, :], dual_ref.at[index], sems.at[index]
        )
        for index in range(MOMS * TIMES)
    ]
    copies.append(pltpu.make_async_copy(sums_hbm, sums_ref, sems.at[MOMS * TIMES]))
    for copy in copies:
        copy.start()
    lane = lax.broadcasted_iota(jnp.int32, (64, 128), 1)
    upper = (lax.broadcasted_iota(jnp.int32, (1024, 128), 0) & 4) == 0
    total = jnp.zeros((64, 128), F32)
    for index in range(MOMS * TIMES):
        copies[index].wait()
        got = got_ref[:, index * 16 : (index + 1) * 16, :].reshape(1024, 128)
        other = dual_ref[index].reshape(1024, 128)
        real = jnp.sum(got * other)
        turned = jnp.where(upper, -pltpu.roll(other, 1020, 0), pltpu.roll(other, 4, 0))
        imag = jnp.sum(got * turned)
        total += jnp.where(lane == index, real, 0.0) + jnp.where(lane == index + 4, imag, 0.0)
    copies[-1].wait()
    total_ref[...] = total + sums_ref[...]


def meet(got, other, sums):
    hbm = pl.BlockSpec(memory_space=pltpu.HBM)
    return pl.pallas_call(
        meet_body,
        in_specs=[VMEM, hbm, hbm],
        out_specs=VMEM,
        out_shape=jax.ShapeDtypeStruct((64, 128), F32),
        scratch_shapes=[
            pltpu.VMEM((MOMS * TIMES, 64, 16, 128), F32),
            pltpu.VMEM((64, 128), F32),
            pltpu.SemaphoreType.DMA((MOMS * TIMES + 1,)),
        ],
        compiler_params=pltpu.CompilerParams(vmem_limit_bytes=8 << 20),
        **params(1 << 21, 4 << 20),
    )(got, other, sums)


def empty_body(out_ref):
    del out_ref


def shards(elementals, perambulators, owners, pairing):
    slab = elementals.shape[2]
    quarter = lax.axis_index("mom").astype(jnp.int32)

    mine = perambulators[0].reshape(TIMES, 2, 64, 4, N)
    mine = lax.dynamic_index_in_dim(mine, quarter, 3, keepdims=False)
    mine = mine.reshape(4, 64, N).transpose(1, 0, 2)
    pieces = lax.all_to_all(mine, "modes", 0, 0, tiled=True)
    piece = jnp.concatenate(
        [
            lax.dynamic_slice(pieces, (owners[time], 2 * time, 0), (1, 2, N))
            for time in range(TIMES)
        ],
        axis=1,
    )
    own = lax.all_to_all(jnp.broadcast_to(piece, (64, 4, N)), "modes", 0, 0, tiled=True)
    own = own.transpose(1, 0, 2)
    by_core = lax.ppermute(own, "mom", [(i ^ 1, i) for i in range(4)])
    by_chip = lax.ppermute(own, "mom", [(i ^ 2, i) for i in range(4)])
    by_both = lax.ppermute(by_chip, "mom", [(i ^ 1, i) for i in range(4)])
    quarters = [own, by_core, by_chip, by_both]

    high, low = turn(elementals)
    tables = weights(quarter[None], quarters)
    out = pl.pallas_call(
        empty_body,
        out_shape=jax.ShapeDtypeStruct((2, MOMS, TIMES, slab, N, N), BF16),
        out_specs=ANY,
    )()
    sums = jnp.zeros((64, 128), F32)
    other = dual((quarter ^ 3)[None], pairing, tables, high, low)
    for name, group in enumerate(((0,), (1, 2), (3,))):
        sent = first([quarters[shift] for shift in group], high, low)
        got = lax.all_to_all(sent, "modes", 0, 0, tiled=True)
        if name < 2:
            for which, shift in enumerate(group):
                row = (quarter ^ shift)[None]
                out, sums = last(row, pairing, got, len(group), which, tables, high, low, sums, out)
    sums = meet(got, other, sums)
    sums = lax.all_to_all(sums, "modes", 0, 0, tiled=True)
    out, _ = last((quarter ^ 3)[None], pairing, got, 1, 0, tables, high, low, None, out)
    correlator = jnp.sum(sums[:, :8], axis=0).reshape(2, MOMS, TIMES) * float(N) ** -1.5
    return out, correlator


def solution(mesh):
    placed = (
        P(None, "mom", "modes", None, None),
        P("modes", None, None, None, None),
        P(),
        P("mom"),
    )
    return jax.shard_map(
        shards,
        mesh=mesh,
        in_specs=placed,
        out_specs=(P(None, "mom", None, "modes", None, None), P(None, "mom", None)),
        check_vma=False,
    )
```

time: 359 us -> 324 us (0.903)
  Pallas kernels: 60.6 us -> 92.5 us
  waiting for transfers between devices: 183 us -> 161 us
  local copies, waits for them, and re-layouts: 30.4 us -> 11.3 us
  blocking collectives: 17.4 us -> 0 us
  starting transfers between devices: 61.7 us -> 54.1 us
    ppermute x3, waiting for transfers between devices: 146 us -> 50.7 us  [the longest x1 49.2 us: shards(): by_chip = lax.ppermute(own, 'mom', [(i ^ 2, i) for i in range(4)])]
    all_to_all x4 -> x3, waiting for transfers between devices: 17 us -> 90.3 us  [shards(): got = lax.all_to_all(sent, 'modes', 0, 0, tiled=True)]
    pallas_call x9 -> x10, Pallas kernels: 58.5 us -> 85.1 us  [the longest x4 43.5 us: last(): pl.pallas_call(last_body, grid_spec=pltpu.PrefetchScalarGridSpec(num_scal...]
    unnamed x53 -> x21, local copies, waits for them, and re-layouts: 25.6 us -> 5.24 us
    all_to_all x1 -> x0, blocking collectives: 17.4 us -> none  [shards(): sums = lax.all_to_all(sums, 'modes', 0, 0, tiled=True)]
    all_to_all x4 -> x3, starting transfers between devices: 41.9 us -> 24.9 us  [shards(): got = lax.all_to_all(sent, 'modes', 0, 0, tiled=True)]
    all_to_all x0 -> x1, starting transfers between devices: none -> 9.67 us  [shards(): sums = lax.all_to_all(sums, 'modes', 0, 0, tiled=True)]
    pallas_call x1, Pallas kernels: 2.07 us -> 7.35 us  [turn(): pl.pallas_call(turn_body, grid=(MOMS, slab), out_shape=[out, out], in_spe...]
  transfers between devices with their start and end apart: 9 -> 9, of which waited for: 6 -> 7; matrix products, arithmetic and copies ran while one was open for 0% -> 0% of each run, Pallas kernels for 13% -> 26%
where the time goes in v2:
time: 324 us; the launch traced here: 323 us
  waiting for transfers between devices  161 us (50%)
  Pallas kernels  92.5 us (29%)
  starting transfers between devices  54.1 us (17%)
  local copies, waits for them, and re-layouts  11.3 us (3%)
  between operations  4.57 us (1%)
    all_to_all x3, waiting for transfers between devices, shards(): got = lax.all_to_all(sent, 'modes', 0, 0, tiled=True)  90.3 us
    ppermute x1, waiting for transfers between devices, shards(): by_chip = lax.ppermute(own, 'mom', [(i ^ 2, i) for i in range(4)])  49.2 us
    pallas_call x4, Pallas kernels, last(): pl.pallas_call(last_body, grid_spec=pltpu.PrefetchScalarGridSpec(num_scal...  43.5 us
    pallas_call x3, Pallas kernels, first(): pl.pallas_call(functools.partial(first_body, count), in_specs=[VMEM] * co...  25.6 us
    all_to_all x3, starting transfers between devices, shards(): got = lax.all_to_all(sent, 'modes', 0, 0, tiled=True)  24.9 us
    all_to_all x1, starting transfers between devices, shards(): pieces = lax.all_to_all(mine, 'modes', 0, 0, tiled=True)  13.7 us
    all_to_all x1, waiting for transfers between devices, shards(): pieces = lax.all_to_all(mine, 'modes', 0, 0, tiled=True)  11 us
    all_to_all x1, starting transfers between devices, shards(): sums = lax.all_to_all(sums, 'modes', 0, 0, tiled=True)  9.67 us
  transfers between devices with their start and end apart: 9, of which 7 were waited for; matrix products, arithmetic and copies ran while one was open for 0% of the time, Pallas kernels for 26%

profile of v2, /device:TPU:32, one launch (start us, length us, event | category | flops | bytes accessed | tf_op | source)
XLA Modules:
  0.0 323.2 jit_solution(10754798561825586352)
XLA Ops:
  0.6 0.0 copy-start.6
  0.6 1.5 reshape_squeeze.3
  2.2 0.3 constant_dynamic-slice_fusion.2
  2.5 0.9 copy.18
  3.4 13.7 %all-to-all-start = ((f32[64,4,256]{2,1,0:T(4,128)}), f32[64,4,256]{2,1,0:T(4,128)S(1)}, u32[]{:S(2)}, u32[]{:S(2)}) async-start(f32[64,4,256]{2,1,0:T(4,128)} %bitcast.19), calls=%async_computation | async-start | bytes 524288 | tf_op jit(solution)/shard_map/all_to_all | solution.py:332
  17.0 0.0 copy-done.6
  17.0 0.6 fusion
  21.4 11.0 %all-to-all-done = f32[64,4,256]{2,1,0:T(4,128)S(1)} async-done(((f32[64,4,256]{2,1,0:T(4,128)}), f32[64,4,256]{2,1,0:T(4,128)S(1)}, u32[]{:S(2)}, u32[]{:S(2)}) %all-to-all-start) | async-done | bytes 262176 | tf_op jit(solution)/shard_map/all_to_all | solution.py:332
  32.4 0.7 broadcast_in_dim.26
  33.2 4.6 %all-to-all-start.1 = ((f32[64,4,256]{2,1,0:T(4,128)}), f32[64,4,256]{2,1,0:T(4,128)S(1)}, u32[]{:S(2)}, u32[]{:S(2)}) async-start(f32[64,4,256]{2,1,0:T(4,128)} %broadcast_in_dim.26), calls=%async_computation.1 | async-start | bytes 524288 | tf_op jit(solution)/shard_map/all_to_all | solution.py:340
  37.8 7.4 %shard_map.59 = (bf16[2,4,512,256]{3,2,1,0:T(8,128)(2,1)}, bf16[2,4,512,256]{3,2,1,0:T(8,128)(2,1)}) custom-call(f32[2,2,4,256,256]{4,3,2,1,0:T(8,128)} %elem_ref.1), custom_call_target="tpu_custom_call" | custom-call | flops 1048576 | bytes 8388608 | tf_op jit(solution)/shard_map/pallas_call | solution.py:52
  45.1 7.0 %all-to-all-done.1 = f32[64,4,256]{2,1,0:T(4,128)S(1)} async-done(((f32[64,4,256]{2,1,0:T(4,128)}), f32[64,4,256]{2,1,0:T(4,128)S(1)}, u32[]{:S(2)}, u32[]{:S(2)}) %all-to-all-start.1) | async-done | bytes 262176 | tf_op jit(solution)/shard_map/all_to_all | solution.py:340
  52.1 0.8 copy.19
  52.9 7.3 %shard_map.63 = f32[64,64,128]{2,1,0:T(8,128)} custom-call(f32[4,64,256]{2,1,0:T(8,128)} %bitcast.21, bf16[2,4,512,256]{3,2,1,0:T(8,128)(2,1)} %get-tuple-element.14.refs_1_.refs_2_.refs_0_.high_ref, bf16[2,4,512,256]{3,2,1,0:T(8,128)(2,1)} %get-tuple-element.15.refs_2_.refs_3_.refs_1_.low_ref), custom_call_target="tpu_custom_call" | custom-call | flops 1610612736 | bytes 6291456 | tf_op jit(solution)/shard_map/pallas_call | solution.py:120
  60.2 5.8 %all-to-all-start.4 = ((f32[64,64,128]{2,1,0:T(8,128)}), f32[64,64,128]{2,1,0:T(8,128)S(1)}, u32[]{:S(2)}, u32[]{:S(2)}) async-start(f32[64,64,128]{2,1,0:T(8,128)} %shard_map.63), calls=%async_computation.4 | async-start | bytes 4194304 | tf_op jit(solution)/shard_map/all_to_all | solution.py:358
  66.0 0.0 copy-done.4
  66.0 1.1 collective-permute-start
  67.1 0.0 collective-permute-start.2
  67.1 49.2 %collective-permute-done.g2_ref.refs_1_ = f32[4,64,256]{2,1,0:T(8,128)S(1)} collective-permute-done((f32[4,64,256]{2,1,0:T(8,128)S(1)}, f32[4,64,256]{2,1,0:T(8,128)S(1)}, u32[]{:S(2)}, u32[]{:S(2)}) %collective-permute-start) | collective-permute-done | bytes 262176 | tf_op jit(solution)/shard_map/ppermute | solution.py:343
  116.3 0.0 collective-permute-done.2.g1_ref.refs_0_
  116.3 0.7 copy-done.7
  117.0 0.7 copy-done.9
  117.7 11.1 %shard_map.62 = f32[64,128,128]{2,1,0:T(8,128)} custom-call(f32[4,64,256]{2,1,0:T(8,128)} %copy-done.9, f32[4,64,256]{2,1,0:T(8,128)} %copy-done.7, bf16[2,4,512,256]{3,2,1,0:T(8,128)(2,1)} %get-tuple-element.14.refs_1_.refs_2_.refs_0_.high_ref, bf16[2,4,512,256]{3,2,1,0:T(8,128)(2,1)} %get-tuple-element.15.refs_2_.refs_3_.refs_1_.low_ref), custom_call_target="tpu_custom_call" | custom-call | flops 3221225472 | bytes 6291456 | tf_op jit(solution)/shard_map/pallas_call | solution.py:120
  128.7 0.0 copy-start.8
  128.8 0.0 all-to-all-done.4.got_ref
  128.8 0.0 copy-start.3
  128.8 11.9 %all-to-all-start.3 = ((f32[64,128,128]{2,1,0:T(8,128)}), f32[64,128,128]{2,1,0:T(8,128)}, u32[]{:S(2)}, u32[]{:S(2)}) async-start(f32[64,128,128]{2,1,0:T(8,128)} %shard_map.62), calls=%async_computation.3 | async-start | bytes 8388608 | tf_op jit(solution)/shard_map/all_to_all | solution.py:358
  140.7 0.0 copy-done.8
  140.7 0.1 collective-permute-start.1
  140.8 1.5 collective-permute-done.1.refs_0_.g3_ref
  142.3 0.7 copy-done.5
  143.0 7.3 %shard_map.60 = f32[64,64,128]{2,1,0:T(8,128)} custom-call(f32[4,64,256]{2,1,0:T(8,128)} %copy-done.5, bf16[2,4,512,256]{3,2,1,0:T(8,128)(2,1)} %get-tuple-element.14.refs_1_.refs_2_.refs_0_.high_ref, bf16[2,4,512,256]{3,2,1,0:T(8,128)(2,1)} %get-tuple-element.15.refs_2_.refs_3_.refs_1_.low_ref), custom_call_target="tpu_custom_call" | custom-call | flops 1610612736 | bytes 6291456 | tf_op jit(solution)/shard_map/pallas_call | solution.py:120
  150.3 87.4 %all-to-all-done.3.got_ref = f32[64,128,128]{2,1,0:T(8,128)} async-done(((f32[64,128,128]{2,1,0:T(8,128)}), f32[64,128,128]{2,1,0:T(8,128)}, u32[]{:S(2)}, u32[]{:S(2)}) %all-to-all-start.3) | async-done | bytes 4194336 | tf_op jit(solution)/shard_map/all_to_all | solution.py:358
  237.7 7.2 %all-to-all-start.2 = ((f32[64,64,128]{2,1,0:T(8,128)}), f32[64,64,128]{2,1,0:T(8,128)S(1)}, u32[]{:S(2)}, u32[]{:S(2)}) async-start(f32[64,64,128]{2,1,0:T(8,128)} %shard_map.60), calls=%async_computation.2 | async-start | bytes 4194304 | tf_op jit(solution)/shard_map/all_to_all | solution.py:358
  244.9 4.7 %shard_map.61 = (bf16[2,512,512]{2,1,0:T(8,128)(2,1)}, bf16[2,512,512]{2,1,0:T(8,128)(2,1)}, bf16[2,512,512]{2,1,0:T(8,128)(2,1)}, bf16[2,512,512]{2,1,0:T(8,128)(2,1)}) custom-call(s32[1]{0:T(128)} %bitcast.6.quarter_ref.row_ref, f32[4,64,256]{2,1,0:T(8,128)} %bitcast.22, f32[4,64,256]{2,1,0:T(8,128)} %copy-done.9, f32[4,64,256]{2,1,0:T(8,128)} %copy-done.7, ...), custom_call_target="tpu_custom_call" | custom-call | flops 1073741824 | bytes 5242880 | tf_op jit(solution)/shard_map/pallas_call | solution.py:171
  249.6 8.6 %shard_map.69.dual_hbm = f32[64,64,128]{2,1,0:T(8,128)} custom-call(s32[1]{0:T(128)} %bitcast.row_ref, s32[2]{0:T(128)} %pair_ref.9, bf16[2,512,512]{2,1,0:T(8,128)(2,1)} %get-tuple-element.16.vh_ref, bf16[2,512,512]{2,1,0:T(8,128)(2,1)} %get-tuple-element.17.vl_ref, bf16[2,512,512]{2,1,0:T(8,128)(2,1)} %get-tuple-element.18.wh_ref, ...), custom_call_target="tpu_custom_call" | custom-call | flops 3221225472 | bytes 8388608 | tf_op jit(solution)/shard_map/pallas_call | solution.py:266
  258.2 0.6 broadcast_in_dim.30.refs_2_
  258.8 11.1 %shard_map.65 = (bf16[2,2,2,4,256,256]{5,4,3,2,1,0:T(8,128)(2,1)}, f32[64,128]{1,0:T(8,128)}) custom-call(s32[1]{0:T(128)} %bitcast.6.quarter_ref.row_ref, s32[2]{0:T(128)} %pair_ref.9, f32[64,64,128]{2,1,0:T(8,128)} %copy-done.3, bf16[2,512,512]{2,1,0:T(8,128)(2,1)} %get-tuple-element.16.vh_ref, ...), custom_call_target="tpu_custom_call", output_to_operand_aliasing={{0}: (10, {})} | custom-call | flops 3221225472 | bytes 10485760 | tf_op jit(solution)/shard_map/pallas_call | solution.py:222
  269.9 11.1 %shard_map.66 = (bf16[2,2,2,4,256,256]{5,4,3,2,1,0:T(8,128)(2,1)}, f32[64,128]{1,0:T(8,128)}) custom-call(s32[1]{0:T(128)} %bitcast.8.row_ref, s32[2]{0:T(128)} %pair_ref.9, f32[64,128,128]{2,1,0:T(8,128)} %all-to-all-done.3.got_ref, bf16[2,512,512]{2,1,0:T(8,128)(2,1)} %get-tuple-element.16.vh_ref, ...), custom_call_target="tpu_custom_call", output_to_operand_aliasing={{0}: (10, {})} | custom-call | flops 3221225472 | bytes 10485760 | tf_op jit(solution)/shard_map/pallas_call | solution.py:222
  281.0 11.1 %shard_map.67 = (bf16[2,2,2,4,256,256]{5,4,3,2,1,0:T(8,128)(2,1)}, f32[64,128]{1,0:T(8,128)}) custom-call(s32[1]{0:T(128)} %bitcast.7.row_ref, s32[2]{0:T(128)} %pair_ref.9, f32[64,128,128]{2,1,0:T(8,128)} %all-to-all-done.3.got_ref, bf16[2,512,512]{2,1,0:T(8,128)(2,1)} %get-tuple-element.16.vh_ref, ...), custom_call_target="tpu_custom_call", output_to_operand_aliasing={{0}: (10, {})} | custom-call | flops 3221225472 | bytes 10485760 | tf_op jit(solution)/shard_map/pallas_call | solution.py:222
  292.1 2.9 all-to-all-done.2.got_ref
  295.1 2.3 copy-done.1
  297.4 0.8 copy-done.2
  298.2 2.6 shard_map.70
  300.8 9.7 %all-to-all-start.5 = ((f32[64,1,128]{2,1,0:T(1,128)}), f32[64,1,128]{2,1,0:T(1,128)S(1)}, u32[]{:S(2)}, u32[]{:S(2)}) async-start(f32[64,1,128]{2,1,0:T(1,128)} %bitcast.10), calls=%async_computation.5 | async-start | bytes 65536 | tf_op jit(solution)/shard_map/all_to_all | solution.py:364
  310.5 10.3 %shard_map.68 = bf16[2,2,2,4,256,256]{5,4,3,2,1,0:T(8,128)(2,1)} custom-call(s32[1]{0:T(128)} %bitcast.row_ref, s32[2]{0:T(128)} %pair_ref.9, f32[64,64,128]{2,1,0:T(8,128)} %copy-done, bf16[2,512,512]{2,1,0:T(8,128)(2,1)} %get-tuple-element.16.vh_ref, bf16[2,512,512]{2,1,0:T(8,128)(2,1)} %get-tuple-element.17.vl_ref, ...), custom_call_target="tpu_custom_call", output_to_operand_aliasing={{}: (7, {})} | custom-call | flops 3221225472 | bytes 10485760 | tf_op jit(solution)/shard_map/pallas_call | solution.py:222
  320.8 1.7 all-to-all-done.5
  322.5 0.7 mul.7
  (15 shorter events, 0.1 us)
Async XLA Ops:
  0.6 16.4 %copy-start.6 = (s32[2]{0:T(128)S(1)}, s32[2]{0:T(128)}, u32[]{:S(2)}) copy-start(s32[2]{0:T(128)} %param.6) | copy-start | bytes 28
  3.4 29.0 %all-to-all-start = ((f32[64,4,256]{2,1,0:T(4,128)}), f32[64,4,256]{2,1,0:T(4,128)S(1)}, u32[]{:S(2)}, u32[]{:S(2)}) async-start(f32[64,4,256]{2,1,0:T(4,128)} %bitcast.19), calls=%async_computation | async-start | bytes 524288 | tf_op jit(solution)/shard_map/all_to_all | solution.py:332
  33.2 18.9 %all-to-all-start.1 = ((f32[64,4,256]{2,1,0:T(4,128)}), f32[64,4,256]{2,1,0:T(4,128)S(1)}, u32[]{:S(2)}, u32[]{:S(2)}) async-start(f32[64,4,256]{2,1,0:T(4,128)} %broadcast_in_dim.26), calls=%async_computation.1 | async-start | bytes 524288 | tf_op jit(solution)/shard_map/all_to_all | solution.py:340
  52.9 13.1 %copy-start.4 = (f32[64,4,256]{2,0,1:T(8,128)S(1)}, f32[64,4,256]{2,0,1:T(8,128)}, u32[]{:S(2)}) copy-start(f32[64,4,256]{2,0,1:T(8,128)} %copy.19) | copy-start | bytes 786436
  60.2 68.6 %all-to-all-start.4 = ((f32[64,64,128]{2,1,0:T(8,128)}), f32[64,64,128]{2,1,0:T(8,128)S(1)}, u32[]{:S(2)}, u32[]{:S(2)}) async-start(f32[64,64,128]{2,1,0:T(8,128)} %shard_map.63), calls=%async_computation.4 | async-start | bytes 4194304 | tf_op jit(solution)/shard_map/all_to_all | solution.py:358
  66.0 50.3 %collective-permute-start = (f32[4,64,256]{2,1,0:T(8,128)S(1)}, f32[4,64,256]{2,1,0:T(8,128)S(1)}, u32[]{:S(2)}, u32[]{:S(2)}) collective-permute-start(f32[4,64,256]{2,1,0:T(8,128)S(1)} %bitcast.23), channel_id=1, source_target_pairs={{2,0},{3,1},{0,2},{1,3},{6,4},{7,5},{4,6},{5,7},{10,8},{11,9},{8,1... | collective-permute-start | bytes 786440 | tf_op jit(solution)/shard_map/ppermute | solution.py:343
  67.1 49.2 %collective-permute-start.2 = (f32[4,64,256]{2,1,0:T(8,128)S(1)}, f32[4,64,256]{2,1,0:T(8,128)S(1)}, u32[]{:S(2)}, u32[]{:S(2)}) collective-permute-start(f32[4,64,256]{2,1,0:T(8,128)S(1)} %bitcast.24), channel_id=1, source_target_pairs={{1,0},{0,1},{3,2},{2,3},{5,4},{4,5},{7,6},{6,7},{9,8},{8,9},{11,10... | collective-permute-start | bytes 786440 | tf_op jit(solution)/shard_map/ppermute | solution.py:342
  116.2 0.7 copy-start.7
  117.0 0.7 copy-start.9
  128.7 11.9 %copy-start.8 = (f32[4,64,256]{2,1,0:T(8,128)S(1)}, f32[4,64,256]{2,1,0:T(8,128)}, u32[]{:S(2)}) copy-start(f32[4,64,256]{2,1,0:T(8,128)} %copy-done.7) | copy-start | bytes 786436
  128.8 21.5 %copy-start.3 = (f32[64,64,128]{2,1,0:T(8,128)}, f32[64,64,128]{2,1,0:T(8,128)S(1)}, u32[]{:S(2)}) copy-start(f32[64,64,128]{2,1,0:T(8,128)S(1)} %all-to-all-done.4.got_ref) | copy-start | bytes 6291460
  128.8 108.9 %all-to-all-start.3 = ((f32[64,128,128]{2,1,0:T(8,128)}), f32[64,128,128]{2,1,0:T(8,128)}, u32[]{:S(2)}, u32[]{:S(2)}) async-start(f32[64,128,128]{2,1,0:T(8,128)} %shard_map.62), calls=%async_computation.3 | async-start | bytes 8388608 | tf_op jit(solution)/shard_map/all_to_all | solution.py:358
  140.7 1.6 collective-permute-start.1
  142.3 0.7 copy-start.5
  237.7 57.4 %all-to-all-start.2 = ((f32[64,64,128]{2,1,0:T(8,128)}), f32[64,64,128]{2,1,0:T(8,128)S(1)}, u32[]{:S(2)}, u32[]{:S(2)}) async-start(f32[64,64,128]{2,1,0:T(8,128)} %shard_map.60), calls=%async_computation.2 | async-start | bytes 4194304 | tf_op jit(solution)/shard_map/all_to_all | solution.py:358
  295.0 15.4 %copy-start = (f32[64,64,128]{2,1,0:T(8,128)}, f32[64,64,128]{2,1,0:T(8,128)S(1)}, u32[]{:S(2)}) copy-start(f32[64,64,128]{2,1,0:T(8,128)S(1)} %all-to-all-done.2.got_ref) | copy-start | bytes 6291460
  295.1 2.3 copy-start.1
  297.4 0.8 copy-start.2
  300.8 21.7 %all-to-all-start.5 = ((f32[64,1,128]{2,1,0:T(1,128)}), f32[64,1,128]{2,1,0:T(1,128)S(1)}, u32[]{:S(2)}, u32[]{:S(2)}) async-start(f32[64,1,128]{2,1,0:T(1,128)} %bitcast.10), calls=%async_computation.5 | async-start | bytes 65536 | tf_op jit(solution)/shard_map/all_to_all | solution.py:364

commit v3 on v2

--- a/solution.py
+++ b/solution.py
@@ -29,7 +29,12 @@
 
 def dot3(a, b):
     left = jnp.concatenate([a[0], a[0], a[1]], axis=1)
-    return dot(left, jnp.concatenate([b[0], b[1], b[0]], axis=0))
+    right = jnp.concatenate([b[0], b[1], b[0]], axis=0)
+    if right.shape[1] > N:
+        parts = [dot(left, right[:, col : col + N]) for col in range(0, right.shape[1], N)]
+        return jnp.concatenate(parts, axis=1)
+    half = left.shape[0] // 2
+    return jnp.concatenate([dot(left[:half], right), dot(left[half:], right)], axis=0)
 
 
 def params(flops, nbytes):
@@ -70,9 +75,11 @@
             for which, (src, dst) in enumerate(((high_hbm, high_ref), (low_hbm, low_ref)))
         ]
 
-    def store(mom):
-        rows = pl.ds(mom * count * 32, count * 32)
-        return pltpu.make_async_copy(send_ref.at[mom], send_hbm.at[:, rows, :], out_sems.at[mom])
+    def store(mom, index):
+        rows = pl.ds((mom * count + index) * 32, 32)
+        return pltpu.make_async_copy(
+            send_ref.at[mom, index], send_hbm.at[:, rows, :], out_sems.at[mom, index]
+        )
 
     for mom in range(MOMS):
         for a in range(slab):
@@ -90,29 +97,30 @@
                     wl_ref[row : row + ROWS, col : col + N] = low
 
     for mom in range(MOMS):
-        flat = send_ref.at[mom].reshape(64 * count * 32, 128)
-
-        def step(a, carry, mom=mom, flat=flat):
-            for copy in loads(mom, a):
-                copy.wait()
-            elem = (high_ref[mom, a], low_ref[mom, a])
-            for index in range(count):
-                rows = slice(index * 4 * ROWS, (index + 1) * 4 * ROWS)
-                product = dot3((wh_ref[rows], wl_ref[rows]), elem)
+        for index in range(count):
+            flat = send_ref.at[mom, index].reshape(64 * 32, 128)
+            rows = slice(index * 4 * ROWS, (index + 1) * 4 * ROWS)
+
+            def step(a, carry, mom=mom, index=index, flat=flat, rows=rows):
+                if index == 0:
+                    for copy in loads(mom, a):
+                        copy.wait()
+                product = dot3((wh_ref[rows], wl_ref[rows]), (high_ref[mom, a], low_ref[mom, a]))
                 for time in range(TIMES):
                     for comp in range(2):
                         row = (2 * time + comp) * ROWS
                         for half in range(2):
-                            start = ((index * TIMES + time) * 2 + half) * 8 + comp * 4 + a
-                            flat[pl.ds(start, ROWS, stride=count * 32), :] = product[
+                            start = (time * 2 + half) * 8 + comp * 4 + a
+                            flat[pl.ds(start, ROWS, stride=32), :] = product[
                                 row : row + ROWS, half * 128 : (half + 1) * 128
                             ]
-            return carry
-
-        lax.fori_loop(0, slab, step, 0)
-        store(mom).start()
+                return carry
+
+            lax.fori_loop(0, slab, step, 0)
+            store(mom, index).start()
     for mom in range(MOMS):
-        store(mom).wait()
+        for index in range(count):
+            store(mom, index).wait()
 
 
 def first(perams, high, low):
@@ -125,9 +133,9 @@
         scratch_shapes=[pltpu.VMEM((count * 4 * ROWS, 2 * N), BF16)] * 2
         + [pltpu.VMEM((MOMS, slab, 2 * N, N), BF16)] * 2
         + [
-            pltpu.VMEM((MOMS, 64, count * 32, 128), F32),
+            pltpu.VMEM((MOMS, count, 64, 32, 128), F32),
             pltpu.SemaphoreType.DMA((2, MOMS, slab)),
-            pltpu.SemaphoreType.DMA((MOMS,)),
+            pltpu.SemaphoreType.DMA((MOMS, count)),
         ],
         **params(count * 3 * 2 * 256 * 512 * 256 * 8, 6 << 20),
     )(*perams, high, low)
@@ -205,116 +213,131 @@
     sink_re, sink_im = sink[:N], sink[N:]
     real = jnp.sum(sink_re * re + sink_im * im)
     imag = jnp.sum(sink_re * im - sink_im * re)
-    time, mom = pl.program_id(0), pl.program_id(1)
-    add_sums(sums_ref, total_ref, mom * TIMES + time, (time == 0) & (mom == 0), real, imag)
-
-
-TABLE = pl.BlockSpec((1, 2 * N, 2 * N), lambda t, m, row, pair: (t, 0, 0))
-ELEM = pl.BlockSpec((1, 1, 2 * N, N), lambda t, m, row, pair: (pair[m], row[0], 0, 0))
-
-
-def last(row, pairing, got, count, which, tables, high, low, sums, out):
-    whole = pl.BlockSpec((64, 128), lambda t, m, row, pair: (0, 0))
+    time, which, mom = pl.program_id(0), pl.program_id(1), pl.program_id(2)
+    start = (time == 0) & (which == 0) & (mom == 0)
+    add_sums(sums_ref, total_ref, mom * TIMES + time, start, real, imag)
+
+
+def specs(count):
+    table = pl.BlockSpec((1, 2 * N, 2 * N), lambda t, w, m, rows, pair: (t, 0, 0))
+    elem = pl.BlockSpec((1, 1, 2 * N, N), lambda t, w, m, rows, pair: (pair[m], rows[w], 0, 0))
     block = pl.BlockSpec(
-        (64, 16, 128), lambda t, m, row, pair: (0, (m * count + which) * TIMES + t, 0)
-    )
+        (64, 16, 128), lambda t, w, m, rows, pair: (0, (m * count + w) * TIMES + t, 0)
+    )
+    return [table] * 4, [elem] * 2, block
+
+
+def last(rows, pairing, got, tables, high, low, sums, out):
+    count = rows.shape[0]
+    table, elem, block = specs(count)
+    whole = pl.BlockSpec((64, 128), lambda t, w, m, rows, pair: (0, 0))
     with_sums = sums is not None
     result = pl.pallas_call(
         last_body,
         grid_spec=pltpu.PrefetchScalarGridSpec(
             num_scalar_prefetch=2,
-            grid=(TIMES, MOMS),
-            in_specs=[block] + [TABLE] * 4 + ([ELEM, ELEM, whole] if with_sums else []) + [ANY],
+            grid=(TIMES, count, MOMS),
+            in_specs=[block] + table + (elem + [whole] if with_sums else []) + [ANY],
             out_specs=[
-                pl.BlockSpec((2, 1, 1, 1, N, N), lambda t, m, row, pair: (0, m, t, row[0], 0, 0))
+                pl.BlockSpec(
+                    (2, 1, 1, 1, N, N), lambda t, w, m, rows, pair: (0, m, t, rows[w], 0, 0)
+                )
             ]
             + ([whole] if with_sums else []),
         ),
         out_shape=[jax.ShapeDtypeStruct(out.shape, BF16)]
         + ([jax.ShapeDtypeStruct((64, 128), F32)] if with_sums else []),
         input_output_aliases={10 if with_sums else 7: 0},
-        **params(3 * 2 * 2 * 512 * 512 * 256 * 4, 10 << 20),
-    )(row, pairing, got, *tables, *((high, low, sums) if with_sums else ()), out)
+        **params(count * 3 * 2 * 2 * 512 * 512 * 256 * 4, count * (10 << 20)),
+    )(rows, pairing, got, *tables, *((high, low, sums) if with_sums else ()), out)
     return result if with_sums else (result[0], None)
 
 
-def dual_body(row_ref, pair_ref, vh_ref, vl_ref, wh_ref, wl_ref, high_ref, low_ref, out_ref):
-    del row_ref, pair_ref
+def dual_body(rows_ref, pair_ref, vh_ref, vl_ref, wh_ref, wl_ref, high_ref, low_ref, out_ref):
+    del rows_ref, pair_ref
     high, low = [
         jnp.concatenate([ref[0, 0, :N], ref[0, 0, N:]], axis=1) for ref in (high_ref, low_ref)
     ]
-    second = lax.dot_general(
-        jnp.concatenate([high, high, low], axis=1),
-        jnp.concatenate([vh_ref[0], vl_ref[0], vh_ref[0]], axis=1),
-        (((1,), (1,)), ((), ())),
-        preferred_element_type=F32,
-    )
-    high, low = halves(jnp.concatenate([second[:, :N], second[:, N:]], axis=0))
-    full = lax.dot_general(
-        jnp.concatenate([wh_ref[0], wh_ref[0], wl_ref[0]], axis=0),
-        jnp.concatenate([high, low, high], axis=0),
-        (((0,), (0,)), ((), ())),
-        preferred_element_type=F32,
-    )
-    for half in range(2):
-        out_ref[:, half * 8 : (half + 1) * 8, :] = full[:, half * 128 : (half + 1) * 128].reshape(
-            64, 8, 128
+    left = jnp.concatenate([high, high, low], axis=1)
+    second = []
+    for comp in range(2):
+        rows = slice(comp * N, (comp + 1) * N)
+        right = jnp.concatenate([vh_ref[0, rows], vl_ref[0, rows], vh_ref[0, rows]], axis=1)
+        second.append(
+            lax.dot_general(left, right, (((1,), (1,)), ((), ())), preferred_element_type=F32)
         )
-
-
-def dual(row, pairing, tables, high, low):
+    high, low = halves(jnp.concatenate(second, axis=0))
+    right = jnp.concatenate([high, low, high], axis=0)
+    for part in range(2):
+        cols = slice(part * N, (part + 1) * N)
+        left = jnp.concatenate([wh_ref[0, :, cols], wh_ref[0, :, cols], wl_ref[0, :, cols]], axis=0)
+        full = lax.dot_general(left, right, (((0,), (0,)), ((), ())), preferred_element_type=F32)
+        for half in range(2):
+            out_ref[part * 32 : (part + 1) * 32, half * 8 : (half + 1) * 8, :] = full[
+                :, half * 128 : (half + 1) * 128
+            ].reshape(32, 8, 128)
+
+
+def dual(rows, pairing, tables, high, low):
+    count = rows.shape[0]
+    table, elem, block = specs(count)
     return pl.pallas_call(
         dual_body,
         grid_spec=pltpu.PrefetchScalarGridSpec(
             num_scalar_prefetch=2,
-            grid=(TIMES, MOMS),
-            in_specs=[TABLE] * 4 + [ELEM, ELEM],
-            out_specs=pl.BlockSpec((64, 16, 128), lambda t, m, row, pair: (0, m * TIMES + t, 0)),
+            grid=(TIMES, count, MOMS),
+            in_specs=table + elem,
+            out_specs=block,
         ),
-        out_shape=jax.ShapeDtypeStruct((64, 64, 128), F32),
-        **params(3 * 2 * 2 * 512 * 512 * 256 * 4, 8 << 20),
-    )(row, pairing, *tables, high, low)
-
-
-def meet_body(got_ref, dual_hbm, sums_hbm, total_ref, dual_ref, sums_ref, sems):
-    copies = [
-        pltpu.make_async_copy(
-            dual_hbm.at[:, index * 16 : (index + 1) * 16, :], dual_ref.at[index], sems.at[index]
+        out_shape=jax.ShapeDtypeStruct((64, MOMS * count * TIMES * 16, 128), F32),
+        **params(count * 3 * 2 * 2 * 512 * 512 * 256 * 4, count * (8 << 20)),
+    )(rows, pairing, *tables, high, low)
+
+
+def meet_body(got_hbm, dual_hbm, sums_ref, total_ref, got_ref, dual_ref, sems):
+    steps, share = sems.shape[1], got_ref.shape[0] // sems.shape[1]
+    blocks = got_ref.shape[1] // 16
+    copies = []
+    for step in range(steps):
+        part = pl.ds(step * share, share)
+        copies.append(
+            [
+                pltpu.make_async_copy(src.at[part], dst.at[part], sems.at[which, step])
+                for which, (src, dst) in enumerate(((got_hbm, got_ref), (dual_hbm, dual_ref)))
+            ]
         )
-        for index in range(MOMS * TIMES)
-    ]
-    copies.append(pltpu.make_async_copy(sums_hbm, sums_ref, sems.at[MOMS * TIMES]))
-    for copy in copies:
-        copy.start()
+        for copy in copies[-1]:
+            copy.start()
+    sums = [[jnp.zeros((8, 128), F32)] * (MOMS * TIMES) for _ in range(2)]
+    for step in range(steps):
+        for copy in copies[step]:
+            copy.wait()
+        part = slice(step * share, (step + 1) * share)
+        for block in range(blocks):
+            index = block // (blocks // MOMS) * TIMES + block % TIMES
+            for half in range(2):
+                rows = slice(block * 16 + half * 8, block * 16 + half * 8 + 8)
+                got = got_ref[part, rows, :]
+                other = dual_ref[part, rows, :]
+                sums[0][index] += jnp.sum(got * other, axis=0)
+                sums[1][index] += jnp.sum(got * pltpu.roll(other, 4, 1), axis=0)
+    sign = jnp.where((lax.broadcasted_iota(jnp.int32, (8, 128), 0) & 4) == 0, -1.0, 1.0)
     lane = lax.broadcasted_iota(jnp.int32, (64, 128), 1)
-    upper = (lax.broadcasted_iota(jnp.int32, (1024, 128), 0) & 4) == 0
-    total = jnp.zeros((64, 128), F32)
+    total = sums_ref[...]
     for index in range(MOMS * TIMES):
-        copies[index].wait()
-        got = got_ref[:, index * 16 : (index + 1) * 16, :].reshape(1024, 128)
-        other = dual_ref[index].reshape(1024, 128)
-        real = jnp.sum(got * other)
-        turned = jnp.where(upper, -pltpu.roll(other, 1020, 0), pltpu.roll(other, 4, 0))
-        imag = jnp.sum(got * turned)
-        total += jnp.where(lane == index, real, 0.0) + jnp.where(lane == index + 4, imag, 0.0)
-    copies[-1].wait()
-    total_ref[...] = total + sums_ref[...]
+        total += jnp.where(lane == index, jnp.sum(sums[0][index]), 0.0)
+        total += jnp.where(lane == index + 4, jnp.sum(sign * sums[1][index]), 0.0)
+    total_ref[...] = total
 
 
 def meet(got, other, sums):
-    hbm = pl.BlockSpec(memory_space=pltpu.HBM)
     return pl.pallas_call(
         meet_body,
-        in_specs=[VMEM, hbm, hbm],
+        in_specs=[ANY, ANY, VMEM],
         out_specs=VMEM,
         out_shape=jax.ShapeDtypeStruct((64, 128), F32),
-        scratch_shapes=[
-            pltpu.VMEM((MOMS * TIMES, 64, 16, 128), F32),
-            pltpu.VMEM((64, 128), F32),
-            pltpu.SemaphoreType.DMA((MOMS * TIMES + 1,)),
-        ],
-        compiler_params=pltpu.CompilerParams(vmem_limit_bytes=8 << 20),
-        **params(1 << 21, 4 << 20),
+        scratch_shapes=[pltpu.VMEM(got.shape, F32)] * 2 + [pltpu.SemaphoreType.DMA((2, 8))],
+        **params(1 << 22, 8 << 20),
     )(got, other, sums)
 
 
@@ -352,17 +375,17 @@
         out_specs=ANY,
     )()
     sums = jnp.zeros((64, 128), F32)
-    other = dual((quarter ^ 3)[None], pairing, tables, high, low)
-    for name, group in enumerate(((0,), (1, 2), (3,))):
-        sent = first([quarters[shift] for shift in group], high, low)
-        got = lax.all_to_all(sent, "modes", 0, 0, tiled=True)
-        if name < 2:
-            for which, shift in enumerate(group):
-                row = (quarter ^ shift)[None]
-                out, sums = last(row, pairing, got, len(group), which, tables, high, low, sums, out)
-    sums = meet(got, other, sums)
+    rows = jnp.stack([quarter ^ 2, quarter ^ 3])
+    other = dual(rows, pairing, tables, high, low)
+    gots = []
+    for name in range(2):
+        sent = first(quarters[2 * name : 2 * name + 2], high, low)
+        gots.append(lax.all_to_all(sent, "modes", 0, 0, tiled=True))
+    near = jnp.stack([quarter, quarter ^ 1])
+    out, sums = last(near, pairing, gots[0], tables, high, low, sums, out)
+    sums = meet(gots[1], other, sums)
     sums = lax.all_to_all(sums, "modes", 0, 0, tiled=True)
-    out, _ = last((quarter ^ 3)[None], pairing, got, 1, 0, tables, high, low, None, out)
+    out, _ = last(rows, pairing, gots[1], tables, high, low, None, out)
     correlator = jnp.sum(sums[:, :8], axis=0).reshape(2, MOMS, TIMES) * float(N) ** -1.5
     return out, correlator
 

time: 324 us -> 326 us (level)
  blocking collectives: 0 us -> 18.7 us
  starting transfers between devices: 54.1 us -> 37.9 us
  waiting for transfers between devices: 161 us -> 176 us
  Pallas kernels: 92.5 us -> 79.8 us
  local copies, waits for them, and re-layouts: 11.3 us -> 6.09 us
    ppermute x1, waiting for transfers between devices: 49.2 us -> 96.4 us  [shards(): by_chip = lax.ppermute(own, 'mom', [(i ^ 2, i) for i in range(4)])]
    all_to_all x4 -> x2, waiting for transfers between devices: 97.3 us -> 67.6 us  [shards(): gots.append(lax.all_to_all(sent, 'modes', 0, 0, tiled=True))]
    all_to_all x0 -> x1, blocking collectives: none -> 18.7 us  [shards(): lax.all_to_all(jnp.broadcast_to(piece, (64, 4, N)), 'modes', 0, 0, tiled=...]
    pallas_call x4 -> x2, Pallas kernels: 43.5 us -> 26.8 us  [last(): pl.pallas_call(last_body, grid_spec=pltpu.PrefetchScalarGridSpec(num_scal...]
    all_to_all x4 -> x2, starting transfers between devices: 29.5 us -> 18.5 us  [shards(): gots.append(lax.all_to_all(sent, 'modes', 0, 0, tiled=True))]
    pallas_call x1, Pallas kernels: 8.6 us -> 13.5 us  [dual(): pl.pallas_call(dual_body, grid_spec=pltpu.PrefetchScalarGridSpec(num_scal...]
    all_to_all x1, starting transfers between devices: 9.67 us -> 4.82 us  [shards(): sums = lax.all_to_all(sums, 'modes', 0, 0, tiled=True)]
    unnamed x21 -> x13, local copies, waits for them, and re-layouts: 5.24 us -> 1.45 us
  transfers between devices with their start and end apart: 9 -> 7, of which waited for: 7 -> 4; matrix products, arithmetic and copies ran while one was open for 0% -> 1% of each run, Pallas kernels for 26% -> 20%
where the time goes in v3:
time: 326 us; the launch traced here: 325 us
  waiting for transfers between devices  176 us (54%)
  Pallas kernels  79.8 us (24%)
  starting transfers between devices  37.9 us (12%)
  blocking collectives  18.7 us (6%)
  local copies, waits for them, and re-layouts  6.09 us (2%)
  between operations  4.56 us (1%)
    ppermute x1, waiting for transfers between devices, shards(): by_chip = lax.ppermute(own, 'mom', [(i ^ 2, i) for i in range(4)])  96.4 us
    all_to_all x2, waiting for transfers between devices, shards(): gots.append(lax.all_to_all(sent, 'modes', 0, 0, tiled=True))  67.6 us
    pallas_call x2, Pallas kernels, last(): pl.pallas_call(last_body, grid_spec=pltpu.PrefetchScalarGridSpec(num_scal...  26.8 us
    pallas_call x2, Pallas kernels, first(): pl.pallas_call(functools.partial(first_body, count), in_specs=[VMEM] * co...  22.3 us
    all_to_all x1, blocking collectives, shards(): lax.all_to_all(jnp.broadcast_to(piece, (64, 4, N)), 'modes', 0, 0, tiled=...  18.7 us
    all_to_all x2, starting transfers between devices, shards(): gots.append(lax.all_to_all(sent, 'modes', 0, 0, tiled=True))  18.5 us
    all_to_all x1, starting transfers between devices, shards(): pieces = lax.all_to_all(mine, 'modes', 0, 0, tiled=True)  13.7 us
    pallas_call x1, Pallas kernels, dual(): pl.pallas_call(dual_body, grid_spec=pltpu.PrefetchScalarGridSpec(num_scal...  13.5 us
  transfers between devices with their start and end apart: 7, of which 4 were waited for; matrix products, arithmetic and copies ran while one was open for 1% of the time, Pallas kernels for 20%

profile of v3, /device:TPU:32, one launch (start us, length us, event | category | flops | bytes accessed | tf_op | source)
XLA Modules:
  0.0 324.8 jit_solution(14500704755854145401)
XLA Ops:
  0.6 0.0 copy-start.2
  0.6 1.5 reshape_squeeze.3
  2.2 0.3 constant_dynamic-slice_fusion.2
  2.5 0.9 copy.16
  3.4 13.7 %all-to-all-start = ((f32[64,4,256]{2,1,0:T(4,128)}), f32[64,4,256]{2,1,0:T(4,128)S(1)}, u32[]{:S(2)}, u32[]{:S(2)}) async-start(f32[64,4,256]{2,1,0:T(4,128)} %bitcast.19), calls=%async_computation | async-start | bytes 524288 | tf_op jit(solution)/shard_map/all_to_all | solution.py:355
  17.0 0.0 copy-done.2
  17.0 0.6 fusion
  21.4 11.0 %all-to-all-done = f32[64,4,256]{2,1,0:T(4,128)S(1)} async-done(((f32[64,4,256]{2,1,0:T(4,128)}), f32[64,4,256]{2,1,0:T(4,128)S(1)}, u32[]{:S(2)}, u32[]{:S(2)}) %all-to-all-start) | async-done | bytes 262176 | tf_op jit(solution)/shard_map/all_to_all | solution.py:355
  32.5 18.7 %all_to_all.32 = f32[64,4,256]{2,1,0:T(4,128)S(1)} all-to-all(f32[64,4,256]{2,1,0:T(4,128)S(1)} %broadcast_in_dim.14), channel_id=1, replica_groups=mesh['modes'=64,'mom'=4] {'modes'}, dimensions={0} | all-to-all | bytes 524288 | tf_op jit(solution)/shard_map/all_to_all | solution.py:363
  51.2 0.1 copy.17
  51.2 0.0 copy-start
  51.3 0.1 collective-permute-start.2
  51.4 7.3 %shard_map.59 = (bf16[2,4,512,256]{3,2,1,0:T(8,128)(2,1)}, bf16[2,4,512,256]{3,2,1,0:T(8,128)(2,1)}) custom-call(f32[2,2,4,256,256]{4,3,2,1,0:T(8,128)} %elem_ref.1), custom_call_target="tpu_custom_call" | custom-call | flops 1048576 | bytes 8388608 | tf_op jit(solution)/shard_map/pallas_call | solution.py:57
  58.6 0.0 collective-permute-done.2.g1_ref.refs_1_
  58.6 0.0 copy-start.3
  58.6 0.0 copy-done
  58.6 0.7 copy-done.3
  59.4 11.1 %shard_map.62 = f32[64,128,128]{2,1,0:T(8,128)} custom-call(f32[4,64,256]{2,1,0:T(8,128)} %bitcast.23, f32[4,64,256]{2,1,0:T(8,128)} %copy-done.3, bf16[2,4,512,256]{3,2,1,0:T(8,128)(2,1)} %get-tuple-element.10.refs_2_.refs_0_.high_ref, bf16[2,4,512,256]{3,2,1,0:T(8,128)(2,1)} %get-tuple-element.11.refs_3_.refs_1_.low_ref), custom_call_target="tpu_custom_call" | custom-call | flops 3221225472 | bytes 6291456 | tf_op jit(solution)/shard_map/pallas_call | solution.py:128
  70.5 0.0 copy-start.1
  70.5 5.8 %all-to-all-start.3 = ((f32[64,128,128]{2,1,0:T(8,128)}), f32[64,128,128]{2,1,0:T(8,128)}, u32[]{:S(2)}, u32[]{:S(2)}) async-start(f32[64,128,128]{2,1,0:T(8,128)} %shard_map.62), calls=%async_computation.3 | async-start | bytes 8388608 | tf_op jit(solution)/shard_map/all_to_all | solution.py:383
  76.3 0.0 copy-done.1
  76.3 0.9 collective-permute-start
  77.2 96.4 %collective-permute-done.refs_0_.g2_ref = f32[4,64,256]{2,1,0:T(8,128)S(1)} collective-permute-done((f32[4,64,256]{2,1,0:T(8,128)S(1)}, f32[4,64,256]{2,1,0:T(8,128)S(1)}, u32[]{:S(2)}, u32[]{:S(2)}) %collective-permute-start) | collective-permute-done | bytes 262176 | tf_op jit(solution)/shard_map/ppermute | solution.py:366
  173.6 0.0 copy-start.4
  173.6 0.0 collective-permute-start.1
  173.6 1.5 collective-permute-done.1.refs_1_.g3_ref
  175.2 0.0 copy-done.4
  175.2 0.0 copy-start.5
  175.2 0.7 copy-done.5
  175.9 11.2 %shard_map.60 = f32[64,128,128]{2,1,0:T(8,128)} custom-call(f32[4,64,256]{2,1,0:T(8,128)} %copy-done.4, f32[4,64,256]{2,1,0:T(8,128)} %copy-done.5, bf16[2,4,512,256]{3,2,1,0:T(8,128)(2,1)} %get-tuple-element.10.refs_2_.refs_0_.high_ref, bf16[2,4,512,256]{3,2,1,0:T(8,128)(2,1)} %get-tuple-element.11.refs_3_.refs_1_.low_ref), custom_call_target="tpu_custom_call" | custom-call | flops 3221225472 | bytes 6291456 | tf_op jit(solution)/shard_map/pallas_call | solution.py:128
  187.1 0.0 all-to-all-done.3.got_ref
  187.1 12.7 %all-to-all-start.2 = ((f32[64,128,128]{2,1,0:T(8,128)}), f32[64,128,128]{2,1,0:T(8,128)}, u32[]{:S(2)}, u32[]{:S(2)}) async-start(f32[64,128,128]{2,1,0:T(8,128)} %shard_map.60), calls=%async_computation.2 | async-start | bytes 8388608 | tf_op jit(solution)/shard_map/all_to_all | solution.py:383
  199.8 0.6 pad_add_fusion.row_ref.rows_ref
  200.4 0.6 pad_add_fusion.1.row_ref
  201.0 4.7 %shard_map.61 = (bf16[2,512,512]{2,1,0:T(8,128)(2,1)}, bf16[2,512,512]{2,1,0:T(8,128)(2,1)}, bf16[2,512,512]{2,1,0:T(8,128)(2,1)}, bf16[2,512,512]{2,1,0:T(8,128)(2,1)}) custom-call(s32[1]{0:T(128)} %bitcast.7.quarter_ref, f32[4,64,256]{2,1,0:T(8,128)} %bitcast.24, f32[4,64,256]{2,1,0:T(8,128)} %copy-done.3, f32[4,64,256]{2,1,0:T(8,128)} %copy-done.4, ...), custom_call_target="tpu_custom_call" | custom-call | flops 1073741824 | bytes 5242880 | tf_op jit(solution)/shard_map/pallas_call | solution.py:179
  205.7 13.5 %shard_map.66.dual_hbm = f32[64,128,128]{2,1,0:T(8,128)} custom-call(s32[2]{0:T(128)} %pad_add_fusion.row_ref.rows_ref, s32[2]{0:T(128)} %pair_ref.5, bf16[2,512,512]{2,1,0:T(8,128)(2,1)} %get-tuple-element.12.vh_ref, bf16[2,512,512]{2,1,0:T(8,128)(2,1)} %get-tuple-element.13.vl_ref, bf16[2,512,512]{2,1,0:T(8,128)(2,1)} %get-tuple-element.14.wh_ref, ...), custom_call_target="tpu_custom_call" | custom-call | flops 6442450944 | bytes 16777216 | tf_op jit(solution)/shard_map/pallas_call | solution.py:284
  219.2 0.6 broadcast_in_dim.16.refs_2_
  219.8 14.2 %shard_map.64 = (bf16[2,2,2,4,256,256]{5,4,3,2,1,0:T(8,128)(2,1)}, f32[64,128]{1,0:T(8,128)}) custom-call(s32[2]{0:T(128)} %pad_add_fusion.1.row_ref, s32[2]{0:T(128)} %pair_ref.5, f32[64,128,128]{2,1,0:T(8,128)} %all-to-all-done.3.got_ref, bf16[2,512,512]{2,1,0:T(8,128)(2,1)} %get-tuple-element.12.vh_ref, ...), custom_call_target="tpu_custom_call", output_to_operand_aliasing={{0}: (10, {})} | custom-call | flops 6442450944 | bytes 20971520 | tf_op jit(solution)/shard_map/pallas_call | solution.py:235
  234.0 67.6 %all-to-all-done.2.got_ref.got_hbm = f32[64,128,128]{2,1,0:T(8,128)} async-done(((f32[64,128,128]{2,1,0:T(8,128)}), f32[64,128,128]{2,1,0:T(8,128)}, u32[]{:S(2)}, u32[]{:S(2)}) %all-to-all-start.2) | async-done | bytes 4194336 | tf_op jit(solution)/shard_map/all_to_all | solution.py:383
  301.6 5.1 %shard_map.67 = f32[64,128]{1,0:T(8,128)} custom-call(f32[64,128,128]{2,1,0:T(8,128)} %all-to-all-done.2.got_ref.got_hbm, f32[64,128,128]{2,1,0:T(8,128)} %shard_map.66.dual_hbm, f32[64,128]{1,0:T(8,128)} %get-tuple-element.17.sums_ref), custom_call_target="tpu_custom_call" | custom-call | flops 4194304 | bytes 8388608 | tf_op jit(solution)/shard_map/pallas_call | solution.py:334
  306.7 4.8 %all-to-all-start.4 = ((f32[64,1,128]{2,1,0:T(1,128)}), f32[64,1,128]{2,1,0:T(1,128)S(1)}, u32[]{:S(2)}, u32[]{:S(2)}) async-start(f32[64,1,128]{2,1,0:T(1,128)} %bitcast.26), calls=%async_computation.4 | async-start | bytes 65536 | tf_op jit(solution)/shard_map/all_to_all | solution.py:387
  311.5 12.6 %shard_map.65 = bf16[2,2,2,4,256,256]{5,4,3,2,1,0:T(8,128)(2,1)} custom-call(s32[2]{0:T(128)} %pad_add_fusion.row_ref.rows_ref, s32[2]{0:T(128)} %pair_ref.5, f32[64,128,128]{2,1,0:T(8,128)} %all-to-all-done.2.got_ref.got_hbm, bf16[2,512,512]{2,1,0:T(8,128)(2,1)} %get-tuple-element.12.vh_ref, ...), custom_call_target="tpu_custom_call", output_to_operand_aliasing={{}: (7, {})} | custom-call | flops 6442450944 | bytes 20971520 | tf_op jit(solution)/shard_map/pallas_call | solution.py:235
  324.1 0.0 all-to-all-done.4
  324.1 0.7 mul.7
  (7 shorter events, 0.1 us)
Async XLA Ops:
  0.6 16.4 %copy-start.2 = (s32[2]{0:T(128)S(1)}, s32[2]{0:T(128)}, u32[]{:S(2)}) copy-start(s32[2]{0:T(128)} %param.6) | copy-start | bytes 28
  3.4 29.0 %all-to-all-start = ((f32[64,4,256]{2,1,0:T(4,128)}), f32[64,4,256]{2,1,0:T(4,128)S(1)}, u32[]{:S(2)}, u32[]{:S(2)}) async-start(f32[64,4,256]{2,1,0:T(4,128)} %bitcast.19), calls=%async_computation | async-start | bytes 524288 | tf_op jit(solution)/shard_map/all_to_all | solution.py:355
  51.2 7.4 %copy-start = (f32[64,4,256]{2,0,1:T(8,128)}, f32[64,4,256]{2,0,1:T(8,128)S(1)}, u32[]{:S(2)}) copy-start(f32[64,4,256]{2,0,1:T(8,128)S(1)} %copy.17) | copy-start | bytes 786436
  51.3 7.4 %collective-permute-start.2 = (f32[4,64,256]{2,1,0:T(8,128)S(1)}, f32[4,64,256]{2,1,0:T(8,128)S(1)}, u32[]{:S(2)}, u32[]{:S(2)}) collective-permute-start(f32[4,64,256]{2,1,0:T(8,128)S(1)} %bitcast.22), channel_id=1, source_target_pairs={{1,0},{0,1},{3,2},{2,3},{5,4},{4,5},{7,6},{6,7},{9,8},{8,9},{11,10... | collective-permute-start | bytes 786440 | tf_op jit(solution)/shard_map/ppermute | solution.py:365
  58.6 0.7 copy-start.3
  70.5 5.8 %copy-start.1 = (f32[64,4,256]{2,0,1:T(8,128)S(1)}, f32[64,4,256]{2,0,1:T(8,128)}, u32[]{:S(2)}) copy-start(f32[64,4,256]{2,0,1:T(8,128)} %copy-done) | copy-start | bytes 786436
  70.5 116.6 %all-to-all-start.3 = ((f32[64,128,128]{2,1,0:T(8,128)}), f32[64,128,128]{2,1,0:T(8,128)}, u32[]{:S(2)}, u32[]{:S(2)}) async-start(f32[64,128,128]{2,1,0:T(8,128)} %shard_map.62), calls=%async_computation.3 | async-start | bytes 8388608 | tf_op jit(solution)/shard_map/all_to_all | solution.py:383
  76.3 97.3 %collective-permute-start = (f32[4,64,256]{2,1,0:T(8,128)S(1)}, f32[4,64,256]{2,1,0:T(8,128)S(1)}, u32[]{:S(2)}, u32[]{:S(2)}) collective-permute-start(f32[4,64,256]{2,1,0:T(8,128)S(1)} %bitcast.25), channel_id=1, source_target_pairs={{2,0},{3,1},{0,2},{1,3},{6,4},{7,5},{4,6},{5,7},{10,8},{11,9},{8,1... | collective-permute-start | bytes 786440 | tf_op jit(solution)/shard_map/ppermute | solution.py:366
  173.6 1.5 copy-start.4
  173.6 1.5 collective-permute-start.1
  175.2 0.7 copy-start.5
  187.1 114.5 %all-to-all-start.2 = ((f32[64,128,128]{2,1,0:T(8,128)}), f32[64,128,128]{2,1,0:T(8,128)}, u32[]{:S(2)}, u32[]{:S(2)}) async-start(f32[64,128,128]{2,1,0:T(8,128)} %shard_map.60), calls=%async_computation.2 | async-start | bytes 8388608 | tf_op jit(solution)/shard_map/all_to_all | solution.py:383
  306.7 17.4 %all-to-all-start.4 = ((f32[64,1,128]{2,1,0:T(1,128)}), f32[64,1,128]{2,1,0:T(1,128)S(1)}, u32[]{:S(2)}, u32[]{:S(2)}) async-start(f32[64,1,128]{2,1,0:T(1,128)} %bitcast.26), calls=%async_computation.4 | async-start | bytes 65536 | tf_op jit(solution)/shard_map/all_to_all | solution.py:387

commit v4 on v3

--- a/solution.py
+++ b/solution.py
@@ -25,16 +25,6 @@
 
 def dot(a, b):
     return jnp.dot(a, b, preferred_element_type=F32)
-
-
-def dot3(a, b):
-    left = jnp.concatenate([a[0], a[0], a[1]], axis=1)
-    right = jnp.concatenate([b[0], b[1], b[0]], axis=0)
-    if right.shape[1] > N:
-        parts = [dot(left, right[:, col : col + N]) for col in range(0, right.shape[1], N)]
-        return jnp.concatenate(parts, axis=1)
-    half = left.shape[0] // 2
-    return jnp.concatenate([dot(left[:half], right), dot(left[half:], right)], axis=0)
 
 
 def params(flops, nbytes):
@@ -96,27 +86,27 @@
                     wh_ref[row : row + ROWS, col : col + N] = high
                     wl_ref[row : row + ROWS, col : col + N] = low
 
+    left = jnp.concatenate([wh_ref[...], wh_ref[...], wl_ref[...]], axis=1)
     for mom in range(MOMS):
+        for pair in range(0, slab, 2):
+            products = []
+            for a in (pair, pair + 1):
+                for copy in loads(mom, a):
+                    copy.wait()
+                high, low = high_ref[mom, a], low_ref[mom, a]
+                products.append(dot(left, jnp.concatenate([high, low, high], axis=0)))
+            for a, product in zip((pair, pair + 1), products):
+                for index in range(count):
+                    flat = send_ref.at[mom, index].reshape(64 * 32, 128)
+                    for time in range(TIMES):
+                        for comp in range(2):
+                            row = ((index * TIMES + time) * 2 + comp) * ROWS
+                            for half in range(2):
+                                start = (time * 2 + half) * 8 + comp * 4 + a
+                                flat[pl.ds(start, ROWS, stride=32), :] = product[
+                                    row : row + ROWS, half * 128 : (half + 1) * 128
+                                ]
         for index in range(count):
-            flat = send_ref.at[mom, index].reshape(64 * 32, 128)
-            rows = slice(index * 4 * ROWS, (index + 1) * 4 * ROWS)
-
-            def step(a, carry, mom=mom, index=index, flat=flat, rows=rows):
-                if index == 0:
-                    for copy in loads(mom, a):
-                        copy.wait()
-                product = dot3((wh_ref[rows], wl_ref[rows]), (high_ref[mom, a], low_ref[mom, a]))
-                for time in range(TIMES):
-                    for comp in range(2):
-                        row = (2 * time + comp) * ROWS
-                        for half in range(2):
-                            start = (time * 2 + half) * 8 + comp * 4 + a
-                            flat[pl.ds(start, ROWS, stride=32), :] = product[
-                                row : row + ROWS, half * 128 : (half + 1) * 128
-                            ]
-                return carry
-
-            lax.fori_loop(0, slab, step, 0)
             store(mom, index).start()
     for mom in range(MOMS):
         for index in range(count):
@@ -185,37 +175,54 @@
     )(quarter, *pieces)
 
 
-def add_sums(sums_ref, total_ref, index, start, real, imag):
-    @pl.when(start)
+def last_body(with_sums, row_ref, pair_ref, *refs):
+    del row_ref, pair_ref
+    gots, refs = refs[:MOMS], refs[MOMS:]
+    vh_ref, vl_ref, wh_ref, wl_ref = refs[:4]
+    out_ref = refs[-2] if with_sums else refs[-1]
+    left = jnp.concatenate([wh_ref[0], wh_ref[0], wl_ref[0]], axis=1)
+    seconds = []
+    for got_ref in gots:
+        got = jnp.concatenate(
+            [got_ref[:, half * 8 : (half + 1) * 8, :].reshape(512, 128) for half in range(2)],
+            axis=1,
+        )
+        high, low = halves(got)
+        seconds.append(dot(left, jnp.concatenate([high, low, high], axis=0)))
+    rows = []
+    for second in seconds:
+        high, low = [jnp.concatenate([part[:N], part[N:]], axis=1) for part in halves(second)]
+        rows.append(jnp.concatenate([high, high, low], axis=1))
+    left = jnp.concatenate(rows, axis=0)
+    fulls = []
+    for comp in range(2):
+        cols = slice(comp * N, (comp + 1) * N)
+        right = [vh_ref[0, :, cols], vl_ref[0, :, cols], vh_ref[0, :, cols]]
+        fulls.append(dot(left, jnp.concatenate(right, axis=0)))
+    for mom in range(MOMS):
+        for comp in range(2):
+            out_ref[comp, mom, 0, 0] = fulls[comp][mom * N : (mom + 1) * N].astype(BF16)
+    if not with_sums:
+        return
+    elems, (sums_ref, _, _, total_ref) = refs[4 : 4 + 2 * MOMS], refs[4 + 2 * MOMS :]
+    time, which = pl.program_id(0), pl.program_id(1)
+
+    @pl.when((time == 0) & (which == 0))
     def _():
         total_ref[...] = sums_ref[...]
 
     lane = lax.broadcasted_iota(jnp.int32, (64, 128), 1)
-    total_ref[...] += jnp.where(lane == index, real, 0.0) + jnp.where(lane == index + 4, imag, 0.0)
-
-
-def last_body(row_ref, pair_ref, got_ref, vh_ref, vl_ref, wh_ref, wl_ref, *refs):
-    del row_ref, pair_ref
-    out_ref = refs[-1] if len(refs) == 2 else refs[-2]
-    got = jnp.concatenate(
-        [got_ref[:, half * 8 : (half + 1) * 8, :].reshape(512, 128) for half in range(2)], axis=1
-    )
-    second = dot3((wh_ref[0], wl_ref[0]), halves(got))
-    high, low = [jnp.concatenate([part[:N], part[N:]], axis=1) for part in halves(second)]
-    full = dot3((high, low), (vh_ref[0], vl_ref[0]))
-    re, im = full[:, :N], full[:, N:]
-    out_ref[0, 0, 0, 0] = re.astype(BF16)
-    out_ref[1, 0, 0, 0] = im.astype(BF16)
-    if len(refs) == 2:
-        return
-    high_ref, low_ref, sums_ref, _, _, total_ref = refs
-    sink = high_ref[0, 0].astype(F32) + low_ref[0, 0].astype(F32)
-    sink_re, sink_im = sink[:N], sink[N:]
-    real = jnp.sum(sink_re * re + sink_im * im)
-    imag = jnp.sum(sink_re * im - sink_im * re)
-    time, which, mom = pl.program_id(0), pl.program_id(1), pl.program_id(2)
-    start = (time == 0) & (which == 0) & (mom == 0)
-    add_sums(sums_ref, total_ref, mom * TIMES + time, start, real, imag)
+    total = total_ref[...]
+    for mom in range(MOMS):
+        high_ref, low_ref = elems[mom], elems[MOMS + mom]
+        sink = high_ref[0, 0].astype(F32) + low_ref[0, 0].astype(F32)
+        sink_re, sink_im = sink[:N], sink[N:]
+        re, im = [full[mom * N : (mom + 1) * N] for full in fulls]
+        real = jnp.sum(sink_re * re + sink_im * im)
+        imag = jnp.sum(sink_re * im - sink_im * re)
+        index = mom * TIMES + time
+        total += jnp.where(lane == index, real, 0.0) + jnp.where(lane == index + 4, imag, 0.0)
+    total_ref[...] = total
 
 
 def specs(count):
@@ -229,27 +236,36 @@
 
 def last(rows, pairing, got, tables, high, low, sums, out):
     count = rows.shape[0]
-    table, elem, block = specs(count)
-    whole = pl.BlockSpec((64, 128), lambda t, w, m, rows, pair: (0, 0))
+    table = pl.BlockSpec((1, 2 * N, 2 * N), lambda t, w, rows, pair: (t, 0, 0))
+    whole = pl.BlockSpec((64, 128), lambda t, w, rows, pair: (0, 0))
+    blocks = [
+        pl.BlockSpec((64, 16, 128), lambda t, w, rows, pair, m=m: (0, (m * count + w) * TIMES + t, 0))
+        for m in range(MOMS)
+    ]
+    elems = [
+        pl.BlockSpec((1, 1, 2 * N, N), lambda t, w, rows, pair, m=m: (pair[m], rows[w], 0, 0))
+        for m in range(MOMS)
+    ]
     with_sums = sums is not None
+    extra = (*[high] * MOMS, *[low] * MOMS, sums) if with_sums else ()
     result = pl.pallas_call(
-        last_body,
+        functools.partial(last_body, with_sums),
         grid_spec=pltpu.PrefetchScalarGridSpec(
             num_scalar_prefetch=2,
-            grid=(TIMES, count, MOMS),
-            in_specs=[block] + table + (elem + [whole] if with_sums else []) + [ANY],
+            grid=(TIMES, count),
+            in_specs=blocks + [table] * 4 + (elems + elems + [whole] if with_sums else []) + [ANY],
             out_specs=[
                 pl.BlockSpec(
-                    (2, 1, 1, 1, N, N), lambda t, w, m, rows, pair: (0, m, t, rows[w], 0, 0)
+                    (2, MOMS, 1, 1, N, N), lambda t, w, rows, pair: (0, 0, t, rows[w], 0, 0)
                 )
             ]
             + ([whole] if with_sums else []),
         ),
         out_shape=[jax.ShapeDtypeStruct(out.shape, BF16)]
         + ([jax.ShapeDtypeStruct((64, 128), F32)] if with_sums else []),
-        input_output_aliases={10 if with_sums else 7: 0},
+        input_output_aliases={2 + MOMS + 4 + len(extra): 0},
         **params(count * 3 * 2 * 2 * 512 * 512 * 256 * 4, count * (10 << 20)),
-    )(rows, pairing, got, *tables, *((high, low, sums) if with_sums else ()), out)
+    )(rows, pairing, *[got] * MOMS, *tables, *extra, out)
     return result if with_sums else (result[0], None)
 
 

time: 326 us -> 332 us (1.018)
  Pallas kernels: 79.8 us -> 83.2 us
    pallas_call x2, Pallas kernels: 22.3 us -> 28.6 us  [first(): pl.pallas_call(functools.partial(first_body, count), in_specs=[VMEM] * co...]
  transfers between devices with their start and end apart: 7 -> 7, of which waited for: 4 -> 5; matrix products, arithmetic and copies ran while one was open for 1% -> 1% of each run, Pallas kernels for 20% -> 19%
where the time goes in v4:
time: 332 us; the launch traced here: 331 us
  waiting for transfers between devices  179 us (54%)
  Pallas kernels  83.2 us (25%)
  starting transfers between devices  38.2 us (12%)
  blocking collectives  18.7 us (6%)
  local copies, waits for them, and re-layouts  6.09 us (2%)
  between operations  4.56 us (1%)
    ppermute x1, waiting for transfers between devices, shards(): by_chip = lax.ppermute(own, 'mom', [(i ^ 2, i) for i in range(4)])  96.8 us
    all_to_all x2, waiting for transfers between devices, shards(): gots.append(lax.all_to_all(sent, 'modes', 0, 0, tiled=True))  68.9 us
    pallas_call x2, Pallas kernels, first(): pl.pallas_call(functools.partial(first_body, count), in_specs=[VMEM] * co...  28.6 us
    pallas_call x2, Pallas kernels, last(): pl.pallas_call(functools.partial(last_body, with_sums), grid_spec=pltpu.P...  24 us
    all_to_all x1, blocking collectives, shards(): lax.all_to_all(jnp.broadcast_to(piece, (64, 4, N)), 'modes', 0, 0, tiled=...  18.7 us
    all_to_all x2, starting transfers between devices, shards(): gots.append(lax.all_to_all(sent, 'modes', 0, 0, tiled=True))  18 us
    all_to_all x1, starting transfers between devices, shards(): pieces = lax.all_to_all(mine, 'modes', 0, 0, tiled=True)  13.7 us
    pallas_call x1, Pallas kernels, dual(): pl.pallas_call(dual_body, grid_spec=pltpu.PrefetchScalarGridSpec(num_scal...  13.5 us
  transfers between devices with their start and end apart: 7, of which 5 were waited for; matrix products, arithmetic and copies ran while one was open for 1% of the time, Pallas kernels for 19%

profile of v4, /device:TPU:32, one launch (start us, length us, event | category | flops | bytes accessed | tf_op | source)
XLA Modules:
  0.0 331.4 jit_solution(8709596683857606087)
XLA Ops:
  0.6 0.0 copy-start.2
  0.6 1.5 reshape_squeeze.3
  2.2 0.3 constant_dynamic-slice_fusion.2
  2.5 0.9 copy.16
  3.4 13.7 %all-to-all-start = ((f32[64,4,256]{2,1,0:T(4,128)}), f32[64,4,256]{2,1,0:T(4,128)S(1)}, u32[]{:S(2)}, u32[]{:S(2)}) async-start(f32[64,4,256]{2,1,0:T(4,128)} %bitcast.19), calls=%async_computation | async-start | bytes 524288 | tf_op jit(solution)/shard_map/all_to_all | solution.py:371
  17.0 0.0 copy-done.2
  17.0 0.6 fusion
  21.4 11.0 %all-to-all-done = f32[64,4,256]{2,1,0:T(4,128)S(1)} async-done(((f32[64,4,256]{2,1,0:T(4,128)}), f32[64,4,256]{2,1,0:T(4,128)S(1)}, u32[]{:S(2)}, u32[]{:S(2)}) %all-to-all-start) | async-done | bytes 262176 | tf_op jit(solution)/shard_map/all_to_all | solution.py:371
  32.5 18.7 %all_to_all.32 = f32[64,4,256]{2,1,0:T(4,128)S(1)} all-to-all(f32[64,4,256]{2,1,0:T(4,128)S(1)} %broadcast_in_dim.14), channel_id=1, replica_groups=mesh['modes'=64,'mom'=4] {'modes'}, dimensions={0} | all-to-all | bytes 524288 | tf_op jit(solution)/shard_map/all_to_all | solution.py:379
  51.2 0.1 copy.17
  51.2 0.0 copy-start
  51.3 0.1 collective-permute-start.2
  51.4 7.3 %shard_map.59 = (bf16[2,4,512,256]{3,2,1,0:T(8,128)(2,1)}, bf16[2,4,512,256]{3,2,1,0:T(8,128)(2,1)}) custom-call(f32[2,2,4,256,256]{4,3,2,1,0:T(8,128)} %elem_ref.1), custom_call_target="tpu_custom_call" | custom-call | flops 1048576 | bytes 8388608 | tf_op jit(solution)/shard_map/pallas_call | solution.py:47
  58.6 0.0 collective-permute-done.2.g1_ref.refs_1_
  58.6 0.0 copy-start.3
  58.6 0.0 copy-done
  58.6 0.7 copy-done.3
  59.4 14.3 %shard_map.62 = f32[64,128,128]{2,1,0:T(8,128)} custom-call(f32[4,64,256]{2,1,0:T(8,128)} %bitcast.23, f32[4,64,256]{2,1,0:T(8,128)} %copy-done.3, bf16[2,4,512,256]{3,2,1,0:T(8,128)(2,1)} %get-tuple-element.10.refs_2_.refs_6_.refs_7_.high_ref, bf16[2,4,512,256]{3,2,1,0:T(8,128)(2,1)} %get-tuple-element.11.refs_3_.refs_8_.refs_9_.low_ref), custom_call_target="tpu_custom_call" | custom-call | flops 3221225472 | bytes 6291456 | tf_op jit(solution)/shard_map/pallas_call | solution.py:118
  73.6 0.0 copy-start.1
  73.6 5.8 %all-to-all-start.3 = ((f32[64,128,128]{2,1,0:T(8,128)}), f32[64,128,128]{2,1,0:T(8,128)}, u32[]{:S(2)}, u32[]{:S(2)}) async-start(f32[64,128,128]{2,1,0:T(8,128)} %shard_map.62), calls=%async_computation.3 | async-start | bytes 8388608 | tf_op jit(solution)/shard_map/all_to_all | solution.py:399
  79.4 0.0 copy-done.1
  79.5 0.9 collective-permute-start
  80.3 96.8 %collective-permute-done.refs_0_.g2_ref = f32[4,64,256]{2,1,0:T(8,128)S(1)} collective-permute-done((f32[4,64,256]{2,1,0:T(8,128)S(1)}, f32[4,64,256]{2,1,0:T(8,128)S(1)}, u32[]{:S(2)}, u32[]{:S(2)}) %collective-permute-start) | collective-permute-done | bytes 262176 | tf_op jit(solution)/shard_map/ppermute | solution.py:382
  177.1 0.0 copy-start.4
  177.1 0.0 collective-permute-start.1
  177.1 1.5 collective-permute-done.1.refs_1_.g3_ref
  178.7 0.0 copy-done.4
  178.7 0.0 copy-start.5
  178.7 0.7 copy-done.5
  179.4 14.3 %shard_map.60 = f32[64,128,128]{2,1,0:T(8,128)} custom-call(f32[4,64,256]{2,1,0:T(8,128)} %copy-done.4, f32[4,64,256]{2,1,0:T(8,128)} %copy-done.5, bf16[2,4,512,256]{3,2,1,0:T(8,128)(2,1)} %get-tuple-element.10.refs_2_.refs_6_.refs_7_.high_ref, bf16[2,4,512,256]{3,2,1,0:T(8,128)(2,1)} %get-tuple-element.11.refs_3_.refs_8_.refs_9_.low_ref), custom_call_target="tpu_custom_call" | custom-call | flops 3221225472 | bytes 6291456 | tf_op jit(solution)/shard_map/pallas_call | solution.py:118
  193.7 0.0 all-to-all-done.3.refs_0_.refs_1_
  193.7 12.2 %all-to-all-start.2 = ((f32[64,128,128]{2,1,0:T(8,128)}), f32[64,128,128]{2,1,0:T(8,128)}, u32[]{:S(2)}, u32[]{:S(2)}) async-start(f32[64,128,128]{2,1,0:T(8,128)} %shard_map.60), calls=%async_computation.2 | async-start | bytes 8388608 | tf_op jit(solution)/shard_map/all_to_all | solution.py:399
  205.9 0.6 pad_add_fusion.row_ref.rows_ref
  206.5 0.6 pad_add_fusion.1.row_ref
  207.1 4.7 %shard_map.61 = (bf16[2,512,512]{2,1,0:T(8,128)(2,1)}, bf16[2,512,512]{2,1,0:T(8,128)(2,1)}, bf16[2,512,512]{2,1,0:T(8,128)(2,1)}, bf16[2,512,512]{2,1,0:T(8,128)(2,1)}) custom-call(s32[1]{0:T(128)} %bitcast.7.quarter_ref, f32[4,64,256]{2,1,0:T(8,128)} %bitcast.24, f32[4,64,256]{2,1,0:T(8,128)} %copy-done.3, f32[4,64,256]{2,1,0:T(8,128)} %copy-done.4, ...), custom_call_target="tpu_custom_call" | custom-call | flops 1073741824 | bytes 5242880 | tf_op jit(solution)/shard_map/pallas_call | solution.py:169
  211.8 13.5 %shard_map.66.dual_hbm = f32[64,128,128]{2,1,0:T(8,128)} custom-call(s32[2]{0:T(128)} %pad_add_fusion.row_ref.rows_ref, s32[2]{0:T(128)} %pair_ref.5, bf16[2,512,512]{2,1,0:T(8,128)(2,1)} %get-tuple-element.12.refs_2_.vh_ref, bf16[2,512,512]{2,1,0:T(8,128)(2,1)} %get-tuple-element.13.refs_3_.vl_ref, bf16[2,512,512]{2,1,0:T(8,128)(2,1)} %get-tuple-element.14.refs_4_.wh_ref, ...), custom_call_target="tpu_custom_call" | custom-call | flops 6442450944 | bytes 16777216 | tf_op jit(solution)/shard_map/pallas_call | solution.py:300
  225.4 0.6 broadcast_in_dim.16.refs_10_
  226.0 13.2 %shard_map.64 = (bf16[2,2,2,4,256,256]{5,4,3,2,1,0:T(8,128)(2,1)}, f32[64,128]{1,0:T(8,128)}) custom-call(s32[2]{0:T(128)} %pad_add_fusion.1.row_ref, s32[2]{0:T(128)} %pair_ref.5, f32[64,128,128]{2,1,0:T(8,128)} %all-to-all-done.3.refs_0_.refs_1_, f32[64,128,128]{2,1,0:T(8,128)} %all-to-all-done.3.refs_0_.refs_1_, ...), custom_call_target="tpu_custom_call", output_to_operand_aliasing={{0}: (13, {})} | custom-call | flops 6442450944 | bytes 20971520 | tf_op jit(solution)/shard_map/pallas_call | solution.py:251
  239.1 68.9 %all-to-all-done.2.refs_0_.refs_1_.got_hbm = f32[64,128,128]{2,1,0:T(8,128)} async-done(((f32[64,128,128]{2,1,0:T(8,128)}), f32[64,128,128]{2,1,0:T(8,128)}, u32[]{:S(2)}, u32[]{:S(2)}) %all-to-all-start.2) | async-done | bytes 4194336 | tf_op jit(solution)/shard_map/all_to_all | solution.py:399
  308.1 5.1 %shard_map.67 = f32[64,128]{1,0:T(8,128)} custom-call(f32[64,128,128]{2,1,0:T(8,128)} %all-to-all-done.2.refs_0_.refs_1_.got_hbm, f32[64,128,128]{2,1,0:T(8,128)} %shard_map.66.dual_hbm, f32[64,128]{1,0:T(8,128)} %get-tuple-element.17.sums_ref), custom_call_target="tpu_custom_call" | custom-call | flops 4194304 | bytes 8388608 | tf_op jit(solution)/shard_map/pallas_call | solution.py:350
  313.2 5.5 %all-to-all-start.4 = ((f32[64,1,128]{2,1,0:T(1,128)}), f32[64,1,128]{2,1,0:T(1,128)S(1)}, u32[]{:S(2)}, u32[]{:S(2)}) async-start(f32[64,1,128]{2,1,0:T(1,128)} %bitcast.26), calls=%async_computation.4 | async-start | bytes 65536 | tf_op jit(solution)/shard_map/all_to_all | solution.py:403
  318.7 10.8 %shard_map.65 = bf16[2,2,2,4,256,256]{5,4,3,2,1,0:T(8,128)(2,1)} custom-call(s32[2]{0:T(128)} %pad_add_fusion.row_ref.rows_ref, s32[2]{0:T(128)} %pair_ref.5, f32[64,128,128]{2,1,0:T(8,128)} %all-to-all-done.2.refs_0_.refs_1_.got_hbm, f32[64,128,128]{2,1,0:T(8,128)} %all-to-all-done.2.refs_0_.refs_1_.got_hbm, ...), custom_call_target="tpu_custom_call", output_to_operand_aliasing={{}: (8, {})} | custom-call | flops 6442450944 | bytes 20971520 | tf_op jit(solution)/shard_map/pallas_call | solution.py:251
  329.5 1.1 all-to-all-done.4
  330.7 0.7 mul.7
  (7 shorter events, 0.1 us)
Async XLA Ops:
  0.6 16.4 %copy-start.2 = (s32[2]{0:T(128)S(1)}, s32[2]{0:T(128)}, u32[]{:S(2)}) copy-start(s32[2]{0:T(128)} %param.6) | copy-start | bytes 28
  3.4 29.0 %all-to-all-start = ((f32[64,4,256]{2,1,0:T(4,128)}), f32[64,4,256]{2,1,0:T(4,128)S(1)}, u32[]{:S(2)}, u32[]{:S(2)}) async-start(f32[64,4,256]{2,1,0:T(4,128)} %bitcast.19), calls=%async_computation | async-start | bytes 524288 | tf_op jit(solution)/shard_map/all_to_all | solution.py:371
  51.2 7.4 %copy-start = (f32[64,4,256]{2,0,1:T(8,128)}, f32[64,4,256]{2,0,1:T(8,128)S(1)}, u32[]{:S(2)}) copy-start(f32[64,4,256]{2,0,1:T(8,128)S(1)} %copy.17) | copy-start | bytes 786436
  51.3 7.4 %collective-permute-start.2 = (f32[4,64,256]{2,1,0:T(8,128)S(1)}, f32[4,64,256]{2,1,0:T(8,128)S(1)}, u32[]{:S(2)}, u32[]{:S(2)}) collective-permute-start(f32[4,64,256]{2,1,0:T(8,128)S(1)} %bitcast.22), channel_id=1, source_target_pairs={{1,0},{0,1},{3,2},{2,3},{5,4},{4,5},{7,6},{6,7},{9,8},{8,9},{11,10... | collective-permute-start | bytes 786440 | tf_op jit(solution)/shard_map/ppermute | solution.py:381
  58.6 0.7 copy-start.3
  73.6 5.8 %copy-start.1 = (f32[64,4,256]{2,0,1:T(8,128)S(1)}, f32[64,4,256]{2,0,1:T(8,128)}, u32[]{:S(2)}) copy-start(f32[64,4,256]{2,0,1:T(8,128)} %copy-done) | copy-start | bytes 786436
  73.6 120.0 %all-to-all-start.3 = ((f32[64,128,128]{2,1,0:T(8,128)}), f32[64,128,128]{2,1,0:T(8,128)}, u32[]{:S(2)}, u32[]{:S(2)}) async-start(f32[64,128,128]{2,1,0:T(8,128)} %shard_map.62), calls=%async_computation.3 | async-start | bytes 8388608 | tf_op jit(solution)/shard_map/all_to_all | solution.py:399
  79.5 97.7 %collective-permute-start = (f32[4,64,256]{2,1,0:T(8,128)S(1)}, f32[4,64,256]{2,1,0:T(8,128)S(1)}, u32[]{:S(2)}, u32[]{:S(2)}) collective-permute-start(f32[4,64,256]{2,1,0:T(8,128)S(1)} %bitcast.25), channel_id=1, source_target_pairs={{2,0},{3,1},{0,2},{1,3},{6,4},{7,5},{4,6},{5,7},{10,8},{11,9},{8,1... | collective-permute-start | bytes 786440 | tf_op jit(solution)/shard_map/ppermute | solution.py:382
  177.1 1.5 copy-start.4
  177.1 1.5 collective-permute-start.1
  178.7 0.7 copy-start.5
  193.7 114.4 %all-to-all-start.2 = ((f32[64,128,128]{2,1,0:T(8,128)}), f32[64,128,128]{2,1,0:T(8,128)}, u32[]{:S(2)}, u32[]{:S(2)}) async-start(f32[64,128,128]{2,1,0:T(8,128)} %shard_map.60), calls=%async_computation.2 | async-start | bytes 8388608 | tf_op jit(solution)/shard_map/all_to_all | solution.py:399
  313.2 17.5 %all-to-all-start.4 = ((f32[64,1,128]{2,1,0:T(1,128)}), f32[64,1,128]{2,1,0:T(1,128)S(1)}, u32[]{:S(2)}, u32[]{:S(2)}) async-start(f32[64,1,128]{2,1,0:T(1,128)} %bitcast.26), calls=%async_computation.4 | async-start | bytes 65536 | tf_op jit(solution)/shard_map/all_to_all | solution.py:403

commit v5 on v4

--- a/solution.py
+++ b/solution.py
@@ -11,6 +11,7 @@
 ROWS = 64
 MOMS = 2
 TIMES = 2
+PITCH = 40
 F32 = jnp.float32
 BF16 = jnp.bfloat16
 VMEM = pl.BlockSpec(memory_space=pltpu.VMEM)
@@ -68,7 +69,7 @@
     def store(mom, index):
         rows = pl.ds((mom * count + index) * 32, 32)
         return pltpu.make_async_copy(
-            send_ref.at[mom, index], send_hbm.at[:, rows, :], out_sems.at[mom, index]
+            send_ref.at[mom, index, :, pl.ds(0, 32), :], send_hbm.at[:, rows, :], out_sems.at[mom, index]
         )
 
     for mom in range(MOMS):
@@ -86,28 +87,39 @@
                     wh_ref[row : row + ROWS, col : col + N] = high
                     wl_ref[row : row + ROWS, col : col + N] = low
 
-    left = jnp.concatenate([wh_ref[...], wh_ref[...], wl_ref[...]], axis=1)
-    for mom in range(MOMS):
-        for pair in range(0, slab, 2):
-            products = []
-            for a in (pair, pair + 1):
-                for copy in loads(mom, a):
-                    copy.wait()
-                high, low = high_ref[mom, a], low_ref[mom, a]
-                products.append(dot(left, jnp.concatenate([high, low, high], axis=0)))
-            for a, product in zip((pair, pair + 1), products):
-                for index in range(count):
-                    flat = send_ref.at[mom, index].reshape(64 * 32, 128)
-                    for time in range(TIMES):
-                        for comp in range(2):
-                            row = ((index * TIMES + time) * 2 + comp) * ROWS
-                            for half in range(2):
-                                start = (time * 2 + half) * 8 + comp * 4 + a
-                                flat[pl.ds(start, ROWS, stride=32), :] = product[
-                                    row : row + ROWS, half * 128 : (half + 1) * 128
-                                ]
-        for index in range(count):
-            store(mom, index).start()
+    flat = send_ref.reshape(MOMS * count * 64 * PITCH, 128)
+
+    def step(turn, carry):
+        mom = turn // (slab // 2)
+        pair = turn % (slab // 2) * 2
+        left = jnp.concatenate([wh_ref[...], wh_ref[...], wl_ref[...]], axis=1)
+        products = []
+        for which in range(2):
+            a = pair + which
+            for copy in loads(mom, a):
+                copy.wait()
+            high, low = high_ref[mom, a], low_ref[mom, a]
+            products.append(dot(left, jnp.concatenate([high, low, high], axis=0)))
+        for which, product in enumerate(products):
+            for index in range(count):
+                for time in range(TIMES):
+                    for comp in range(2):
+                        row = ((index * TIMES + time) * 2 + comp) * ROWS
+                        for half in range(2):
+                            start = (mom * count + index) * 64 * PITCH + (time * 2 + half) * 8
+                            start += comp * 4 + pair + which
+                            flat[pl.ds(start, ROWS, stride=PITCH), :] = product[
+                                row : row + ROWS, half * 128 : (half + 1) * 128
+                            ]
+
+        @pl.when(pair == slab - 2)
+        def _():
+            for index in range(count):
+                store(mom, index).start()
+
+        return carry
+
+    lax.fori_loop(0, MOMS * slab // 2, step, 0)
     for mom in range(MOMS):
         for index in range(count):
             store(mom, index).wait()
@@ -123,7 +135,7 @@
         scratch_shapes=[pltpu.VMEM((count * 4 * ROWS, 2 * N), BF16)] * 2
         + [pltpu.VMEM((MOMS, slab, 2 * N, N), BF16)] * 2
         + [
-            pltpu.VMEM((MOMS, count, 64, 32, 128), F32),
+            pltpu.VMEM((MOMS, count, 64, PITCH, 128), F32),
             pltpu.SemaphoreType.DMA((2, MOMS, slab)),
             pltpu.SemaphoreType.DMA((MOMS, count)),
         ],

time: 332 us -> 325 us (0.979)
  Pallas kernels: 83.2 us -> 77.7 us
    pallas_call x2, Pallas kernels: 28.6 us -> 23 us  [first(): pl.pallas_call(functools.partial(first_body, count), in_specs=[VMEM] * co...]
where the time goes in v5:
time: 325 us; the launch traced here: 324 us
  waiting for transfers between devices  178 us (55%)
  Pallas kernels  77.7 us (24%)
  starting transfers between devices  37.8 us (12%)
  blocking collectives  18.7 us (6%)
  local copies, waits for them, and re-layouts  6.09 us (2%)
  between operations  4.56 us (1%)
    ppermute x1, waiting for transfers between devices, shards(): by_chip = lax.ppermute(own, 'mom', [(i ^ 2, i) for i in range(4)])  96.4 us
    all_to_all x2, waiting for transfers between devices, shards(): gots.append(lax.all_to_all(sent, 'modes', 0, 0, tiled=True))  67.9 us
    pallas_call x2, Pallas kernels, last(): pl.pallas_call(functools.partial(last_body, with_sums), grid_spec=pltpu.P...  24 us
    pallas_call x2, Pallas kernels, first(): pl.pallas_call(functools.partial(first_body, count), in_specs=[VMEM] * co...  23 us
    all_to_all x1, blocking collectives, shards(): lax.all_to_all(jnp.broadcast_to(piece, (64, 4, N)), 'modes', 0, 0, tiled=...  18.7 us
    all_to_all x2, starting transfers between devices, shards(): gots.append(lax.all_to_all(sent, 'modes', 0, 0, tiled=True))  18.4 us
    all_to_all x1, starting transfers between devices, shards(): pieces = lax.all_to_all(mine, 'modes', 0, 0, tiled=True)  13.7 us
    pallas_call x1, Pallas kernels, dual(): pl.pallas_call(dual_body, grid_spec=pltpu.PrefetchScalarGridSpec(num_scal...  13.5 us
  transfers between devices with their start and end apart: 7, of which 5 were waited for; matrix products, arithmetic and copies ran while one was open for 1% of the time, Pallas kernels for 19%

profile of v5, /device:TPU:32, one launch (start us, length us, event | category | flops | bytes accessed | tf_op | source)
XLA Modules:
  0.0 324.1 jit_solution(5453160877730208161)
XLA Ops:
  0.6 0.0 copy-start.2
  0.6 1.5 reshape_squeeze.3
  2.2 0.3 constant_dynamic-slice_fusion.2
  2.5 0.9 copy.16
  3.4 13.7 %all-to-all-start = ((f32[64,4,256]{2,1,0:T(4,128)}), f32[64,4,256]{2,1,0:T(4,128)S(1)}, u32[]{:S(2)}, u32[]{:S(2)}) async-start(f32[64,4,256]{2,1,0:T(4,128)} %bitcast.19), calls=%async_computation | async-start | bytes 524288 | tf_op jit(solution)/shard_map/all_to_all | solution.py:383
  17.0 0.0 copy-done.2
  17.0 0.6 fusion
  21.4 11.0 %all-to-all-done = f32[64,4,256]{2,1,0:T(4,128)S(1)} async-done(((f32[64,4,256]{2,1,0:T(4,128)}), f32[64,4,256]{2,1,0:T(4,128)S(1)}, u32[]{:S(2)}, u32[]{:S(2)}) %all-to-all-start) | async-done | bytes 262176 | tf_op jit(solution)/shard_map/all_to_all | solution.py:383
  32.5 18.7 %all_to_all.32 = f32[64,4,256]{2,1,0:T(4,128)S(1)} all-to-all(f32[64,4,256]{2,1,0:T(4,128)S(1)} %broadcast_in_dim.14), channel_id=1, replica_groups=mesh['modes'=64,'mom'=4] {'modes'}, dimensions={0} | all-to-all | bytes 524288 | tf_op jit(solution)/shard_map/all_to_all | solution.py:391
  51.2 0.1 copy.17
  51.2 0.0 copy-start
  51.3 0.1 collective-permute-start.2
  51.4 7.3 %shard_map.59 = (bf16[2,4,512,256]{3,2,1,0:T(8,128)(2,1)}, bf16[2,4,512,256]{3,2,1,0:T(8,128)(2,1)}) custom-call(f32[2,2,4,256,256]{4,3,2,1,0:T(8,128)} %elem_ref.1), custom_call_target="tpu_custom_call" | custom-call | flops 1048576 | bytes 8388608 | tf_op jit(solution)/shard_map/pallas_call | solution.py:48
  58.6 0.0 collective-permute-done.2.g1_ref.refs_1_
  58.6 0.0 copy-start.3
  58.6 0.0 copy-done
  58.6 0.7 copy-done.3
  59.4 11.5 %shard_map.62 = f32[64,128,128]{2,1,0:T(8,128)} custom-call(f32[4,64,256]{2,1,0:T(8,128)} %bitcast.23, f32[4,64,256]{2,1,0:T(8,128)} %copy-done.3, bf16[2,4,512,256]{3,2,1,0:T(8,128)(2,1)} %get-tuple-element.10.refs_2_.refs_6_.refs_7_.high_ref, bf16[2,4,512,256]{3,2,1,0:T(8,128)(2,1)} %get-tuple-element.11.refs_3_.refs_8_.refs_9_.low_ref), custom_call_target="tpu_custom_call" | custom-call | flops 3221225472 | bytes 6291456 | tf_op jit(solution)/shard_map/pallas_call | solution.py:130
  70.8 0.0 copy-start.1
  70.8 5.8 %all-to-all-start.3 = ((f32[64,128,128]{2,1,0:T(8,128)}), f32[64,128,128]{2,1,0:T(8,128)}, u32[]{:S(2)}, u32[]{:S(2)}) async-start(f32[64,128,128]{2,1,0:T(8,128)} %shard_map.62), calls=%async_computation.3 | async-start | bytes 8388608 | tf_op jit(solution)/shard_map/all_to_all | solution.py:411
  76.7 0.0 copy-done.1
  76.7 0.9 collective-permute-start
  77.6 96.4 %collective-permute-done.refs_0_.g2_ref = f32[4,64,256]{2,1,0:T(8,128)S(1)} collective-permute-done((f32[4,64,256]{2,1,0:T(8,128)S(1)}, f32[4,64,256]{2,1,0:T(8,128)S(1)}, u32[]{:S(2)}, u32[]{:S(2)}) %collective-permute-start) | collective-permute-done | bytes 262176 | tf_op jit(solution)/shard_map/ppermute | solution.py:394
  174.0 0.0 copy-start.4
  174.0 0.0 collective-permute-start.1
  174.0 1.5 collective-permute-done.1.refs_1_.g3_ref
  175.5 0.0 copy-done.4
  175.5 0.0 copy-start.5
  175.5 0.7 copy-done.5
  176.2 11.5 %shard_map.60 = f32[64,128,128]{2,1,0:T(8,128)} custom-call(f32[4,64,256]{2,1,0:T(8,128)} %copy-done.4, f32[4,64,256]{2,1,0:T(8,128)} %copy-done.5, bf16[2,4,512,256]{3,2,1,0:T(8,128)(2,1)} %get-tuple-element.10.refs_2_.refs_6_.refs_7_.high_ref, bf16[2,4,512,256]{3,2,1,0:T(8,128)(2,1)} %get-tuple-element.11.refs_3_.refs_8_.refs_9_.low_ref), custom_call_target="tpu_custom_call" | custom-call | flops 3221225472 | bytes 6291456 | tf_op jit(solution)/shard_map/pallas_call | solution.py:130
  187.7 0.0 all-to-all-done.3.refs_0_.refs_1_
  187.7 12.6 %all-to-all-start.2 = ((f32[64,128,128]{2,1,0:T(8,128)}), f32[64,128,128]{2,1,0:T(8,128)}, u32[]{:S(2)}, u32[]{:S(2)}) async-start(f32[64,128,128]{2,1,0:T(8,128)} %shard_map.60), calls=%async_computation.2 | async-start | bytes 8388608 | tf_op jit(solution)/shard_map/all_to_all | solution.py:411
  200.4 0.6 pad_add_fusion.row_ref.rows_ref
  200.9 0.6 pad_add_fusion.1.row_ref
  201.5 4.7 %shard_map.61 = (bf16[2,512,512]{2,1,0:T(8,128)(2,1)}, bf16[2,512,512]{2,1,0:T(8,128)(2,1)}, bf16[2,512,512]{2,1,0:T(8,128)(2,1)}, bf16[2,512,512]{2,1,0:T(8,128)(2,1)}) custom-call(s32[1]{0:T(128)} %bitcast.7.quarter_ref, f32[4,64,256]{2,1,0:T(8,128)} %bitcast.24, f32[4,64,256]{2,1,0:T(8,128)} %copy-done.3, f32[4,64,256]{2,1,0:T(8,128)} %copy-done.4, ...), custom_call_target="tpu_custom_call" | custom-call | flops 1073741824 | bytes 5242880 | tf_op jit(solution)/shard_map/pallas_call | solution.py:181
  206.3 13.5 %shard_map.66.dual_hbm = f32[64,128,128]{2,1,0:T(8,128)} custom-call(s32[2]{0:T(128)} %pad_add_fusion.row_ref.rows_ref, s32[2]{0:T(128)} %pair_ref.5, bf16[2,512,512]{2,1,0:T(8,128)(2,1)} %get-tuple-element.12.refs_2_.vh_ref, bf16[2,512,512]{2,1,0:T(8,128)(2,1)} %get-tuple-element.13.refs_3_.vl_ref, bf16[2,512,512]{2,1,0:T(8,128)(2,1)} %get-tuple-element.14.refs_4_.wh_ref, ...), custom_call_target="tpu_custom_call" | custom-call | flops 6442450944 | bytes 16777216 | tf_op jit(solution)/shard_map/pallas_call | solution.py:312
  219.8 0.6 broadcast_in_dim.16.refs_10_
  220.4 13.2 %shard_map.64 = (bf16[2,2,2,4,256,256]{5,4,3,2,1,0:T(8,128)(2,1)}, f32[64,128]{1,0:T(8,128)}) custom-call(s32[2]{0:T(128)} %pad_add_fusion.1.row_ref, s32[2]{0:T(128)} %pair_ref.5, f32[64,128,128]{2,1,0:T(8,128)} %all-to-all-done.3.refs_0_.refs_1_, f32[64,128,128]{2,1,0:T(8,128)} %all-to-all-done.3.refs_0_.refs_1_, ...), custom_call_target="tpu_custom_call", output_to_operand_aliasing={{0}: (13, {})} | custom-call | flops 6442450944 | bytes 20971520 | tf_op jit(solution)/shard_map/pallas_call | solution.py:263
  233.6 67.9 %all-to-all-done.2.refs_0_.refs_1_.got_hbm = f32[64,128,128]{2,1,0:T(8,128)} async-done(((f32[64,128,128]{2,1,0:T(8,128)}), f32[64,128,128]{2,1,0:T(8,128)}, u32[]{:S(2)}, u32[]{:S(2)}) %all-to-all-start.2) | async-done | bytes 4194336 | tf_op jit(solution)/shard_map/all_to_all | solution.py:411
  301.5 5.1 %shard_map.67 = f32[64,128]{1,0:T(8,128)} custom-call(f32[64,128,128]{2,1,0:T(8,128)} %all-to-all-done.2.refs_0_.refs_1_.got_hbm, f32[64,128,128]{2,1,0:T(8,128)} %shard_map.66.dual_hbm, f32[64,128]{1,0:T(8,128)} %get-tuple-element.17.sums_ref), custom_call_target="tpu_custom_call" | custom-call | flops 4194304 | bytes 8388608 | tf_op jit(solution)/shard_map/pallas_call | solution.py:362
  306.6 4.8 %all-to-all-start.4 = ((f32[64,1,128]{2,1,0:T(1,128)}), f32[64,1,128]{2,1,0:T(1,128)S(1)}, u32[]{:S(2)}, u32[]{:S(2)}) async-start(f32[64,1,128]{2,1,0:T(1,128)} %bitcast.26), calls=%async_computation.4 | async-start | bytes 65536 | tf_op jit(solution)/shard_map/all_to_all | solution.py:415
  311.4 10.8 %shard_map.65 = bf16[2,2,2,4,256,256]{5,4,3,2,1,0:T(8,128)(2,1)} custom-call(s32[2]{0:T(128)} %pad_add_fusion.row_ref.rows_ref, s32[2]{0:T(128)} %pair_ref.5, f32[64,128,128]{2,1,0:T(8,128)} %all-to-all-done.2.refs_0_.refs_1_.got_hbm, f32[64,128,128]{2,1,0:T(8,128)} %all-to-all-done.2.refs_0_.refs_1_.got_hbm, ...), custom_call_target="tpu_custom_call", output_to_operand_aliasing={{}: (8, {})} | custom-call | flops 6442450944 | bytes 20971520 | tf_op jit(solution)/shard_map/pallas_call | solution.py:263
  322.2 1.1 all-to-all-done.4
  323.4 0.7 mul.7
  (7 shorter events, 0.1 us)
Async XLA Ops:
  0.6 16.4 %copy-start.2 = (s32[2]{0:T(128)S(1)}, s32[2]{0:T(128)}, u32[]{:S(2)}) copy-start(s32[2]{0:T(128)} %param.6) | copy-start | bytes 28
  3.4 29.0 %all-to-all-start = ((f32[64,4,256]{2,1,0:T(4,128)}), f32[64,4,256]{2,1,0:T(4,128)S(1)}, u32[]{:S(2)}, u32[]{:S(2)}) async-start(f32[64,4,256]{2,1,0:T(4,128)} %bitcast.19), calls=%async_computation | async-start | bytes 524288 | tf_op jit(solution)/shard_map/all_to_all | solution.py:383
  51.2 7.4 %copy-start = (f32[64,4,256]{2,0,1:T(8,128)}, f32[64,4,256]{2,0,1:T(8,128)S(1)}, u32[]{:S(2)}) copy-start(f32[64,4,256]{2,0,1:T(8,128)S(1)} %copy.17) | copy-start | bytes 786436
  51.3 7.4 %collective-permute-start.2 = (f32[4,64,256]{2,1,0:T(8,128)S(1)}, f32[4,64,256]{2,1,0:T(8,128)S(1)}, u32[]{:S(2)}, u32[]{:S(2)}) collective-permute-start(f32[4,64,256]{2,1,0:T(8,128)S(1)} %bitcast.22), channel_id=1, source_target_pairs={{1,0},{0,1},{3,2},{2,3},{5,4},{4,5},{7,6},{6,7},{9,8},{8,9},{11,10... | collective-permute-start | bytes 786440 | tf_op jit(solution)/shard_map/ppermute | solution.py:393
  58.6 0.7 copy-start.3
  70.8 5.8 %copy-start.1 = (f32[64,4,256]{2,0,1:T(8,128)S(1)}, f32[64,4,256]{2,0,1:T(8,128)}, u32[]{:S(2)}) copy-start(f32[64,4,256]{2,0,1:T(8,128)} %copy-done) | copy-start | bytes 786436
  70.8 116.9 %all-to-all-start.3 = ((f32[64,128,128]{2,1,0:T(8,128)}), f32[64,128,128]{2,1,0:T(8,128)}, u32[]{:S(2)}, u32[]{:S(2)}) async-start(f32[64,128,128]{2,1,0:T(8,128)} %shard_map.62), calls=%async_computation.3 | async-start | bytes 8388608 | tf_op jit(solution)/shard_map/all_to_all | solution.py:411
  76.7 97.3 %collective-permute-start = (f32[4,64,256]{2,1,0:T(8,128)S(1)}, f32[4,64,256]{2,1,0:T(8,128)S(1)}, u32[]{:S(2)}, u32[]{:S(2)}) collective-permute-start(f32[4,64,256]{2,1,0:T(8,128)S(1)} %bitcast.25), channel_id=1, source_target_pairs={{2,0},{3,1},{0,2},{1,3},{6,4},{7,5},{4,6},{5,7},{10,8},{11,9},{8,1... | collective-permute-start | bytes 786440 | tf_op jit(solution)/shard_map/ppermute | solution.py:394
  174.0 1.5 copy-start.4
  174.0 1.5 collective-permute-start.1
  175.5 0.7 copy-start.5
  187.7 113.7 %all-to-all-start.2 = ((f32[64,128,128]{2,1,0:T(8,128)}), f32[64,128,128]{2,1,0:T(8,128)}, u32[]{:S(2)}, u32[]{:S(2)}) async-start(f32[64,128,128]{2,1,0:T(8,128)} %shard_map.60), calls=%async_computation.2 | async-start | bytes 8388608 | tf_op jit(solution)/shard_map/all_to_all | solution.py:411
  306.6 16.8 %all-to-all-start.4 = ((f32[64,1,128]{2,1,0:T(1,128)}), f32[64,1,128]{2,1,0:T(1,128)S(1)}, u32[]{:S(2)}, u32[]{:S(2)}) async-start(f32[64,1,128]{2,1,0:T(1,128)} %bitcast.26), calls=%async_computation.4 | async-start | bytes 65536 | tf_op jit(solution)/shard_map/all_to_all | solution.py:415

commit v6 on v5

--- a/solution.py
+++ b/solution.py
@@ -72,10 +72,10 @@
             send_ref.at[mom, index, :, pl.ds(0, 32), :], send_hbm.at[:, rows, :], out_sems.at[mom, index]
         )
 
-    for mom in range(MOMS):
-        for a in range(slab):
-            for copy in loads(mom, a):
-                copy.start()
+    order = [(mom, a) for mom in range(MOMS) for a in range(slab)]
+    for place in order[:2]:
+        for copy in loads(*place):
+            copy.start()
     for index, ref in enumerate(perams):
         for time in range(TIMES):
             re = ref[2 * time]
@@ -87,6 +87,9 @@
                     wh_ref[row : row + ROWS, col : col + N] = high
                     wl_ref[row : row + ROWS, col : col + N] = low
 
+    for place in order[2:]:
+        for copy in loads(*place):
+            copy.start()
     flat = send_ref.reshape(MOMS * count * 64 * PITCH, 128)
 
     def step(turn, carry):
@@ -100,8 +103,8 @@
                 copy.wait()
             high, low = high_ref[mom, a], low_ref[mom, a]
             products.append(dot(left, jnp.concatenate([high, low, high], axis=0)))
-        for which, product in enumerate(products):
-            for index in range(count):
+        for index in range(count):
+            for which, product in enumerate(products):
                 for time in range(TIMES):
                     for comp in range(2):
                         row = ((index * TIMES + time) * 2 + comp) * ROWS
@@ -112,9 +115,8 @@
                                 row : row + ROWS, half * 128 : (half + 1) * 128
                             ]
 
-        @pl.when(pair == slab - 2)
-        def _():
-            for index in range(count):
+            @pl.when(pair == slab - 2)
+            def _(index=index):
                 store(mom, index).start()
 
         return carry

time: 325 us -> 327 us (level)
  no operation moved by 1% of the time
where the time goes in v6:
time: 327 us; the launch traced here: 326 us
  waiting for transfers between devices  179 us (55%)
  Pallas kernels  77.8 us (24%)
  starting transfers between devices  38.5 us (12%)
  blocking collectives  18.7 us (6%)
  local copies, waits for them, and re-layouts  6.09 us (2%)
  between operations  4.56 us (1%)
    ppermute x1, waiting for transfers between devices, shards(): by_chip = lax.ppermute(own, 'mom', [(i ^ 2, i) for i in range(4)])  96.5 us
    all_to_all x2, waiting for transfers between devices, shards(): gots.append(lax.all_to_all(sent, 'modes', 0, 0, tiled=True))  68.8 us
    pallas_call x2, Pallas kernels, last(): pl.pallas_call(functools.partial(last_body, with_sums), grid_spec=pltpu.P...  24 us
    pallas_call x2, Pallas kernels, first(): pl.pallas_call(functools.partial(first_body, count), in_specs=[VMEM] * co...  23.1 us
    all_to_all x1, blocking collectives, shards(): lax.all_to_all(jnp.broadcast_to(piece, (64, 4, N)), 'modes', 0, 0, tiled=...  18.7 us
    all_to_all x2, starting transfers between devices, shards(): gots.append(lax.all_to_all(sent, 'modes', 0, 0, tiled=True))  18.5 us
    all_to_all x1, starting transfers between devices, shards(): pieces = lax.all_to_all(mine, 'modes', 0, 0, tiled=True)  13.7 us
    pallas_call x1, Pallas kernels, dual(): pl.pallas_call(dual_body, grid_spec=pltpu.PrefetchScalarGridSpec(num_scal...  13.5 us
  transfers between devices with their start and end apart: 7, of which 5 were waited for; matrix products, arithmetic and copies ran while one was open for 1% of the time, Pallas kernels for 19%

profile of v6, /device:TPU:32, one launch (start us, length us, event | category | flops | bytes accessed | tf_op | source)
XLA Modules:
  0.0 325.9 jit_solution(1684791182835827067)
XLA Ops:
  0.6 0.0 copy-start.2
  0.6 1.5 reshape_squeeze.3
  2.2 0.3 constant_dynamic-slice_fusion.2
  2.5 0.9 copy.16
  3.4 13.7 %all-to-all-start = ((f32[64,4,256]{2,1,0:T(4,128)}), f32[64,4,256]{2,1,0:T(4,128)S(1)}, u32[]{:S(2)}, u32[]{:S(2)}) async-start(f32[64,4,256]{2,1,0:T(4,128)} %bitcast.19), calls=%async_computation | async-start | bytes 524288 | tf_op jit(solution)/shard_map/all_to_all | solution.py:385
  17.0 0.0 copy-done.2
  17.0 0.6 fusion
  21.4 11.0 %all-to-all-done = f32[64,4,256]{2,1,0:T(4,128)S(1)} async-done(((f32[64,4,256]{2,1,0:T(4,128)}), f32[64,4,256]{2,1,0:T(4,128)S(1)}, u32[]{:S(2)}, u32[]{:S(2)}) %all-to-all-start) | async-done | bytes 262176 | tf_op jit(solution)/shard_map/all_to_all | solution.py:385
  32.5 18.7 %all_to_all.32 = f32[64,4,256]{2,1,0:T(4,128)S(1)} all-to-all(f32[64,4,256]{2,1,0:T(4,128)S(1)} %broadcast_in_dim.14), channel_id=1, replica_groups=mesh['modes'=64,'mom'=4] {'modes'}, dimensions={0} | all-to-all | bytes 524288 | tf_op jit(solution)/shard_map/all_to_all | solution.py:393
  51.2 0.1 copy.17
  51.2 0.0 copy-start
  51.3 0.1 collective-permute-start.2
  51.4 7.3 %shard_map.59 = (bf16[2,4,512,256]{3,2,1,0:T(8,128)(2,1)}, bf16[2,4,512,256]{3,2,1,0:T(8,128)(2,1)}) custom-call(f32[2,2,4,256,256]{4,3,2,1,0:T(8,128)} %elem_ref.1), custom_call_target="tpu_custom_call" | custom-call | flops 1048576 | bytes 8388608 | tf_op jit(solution)/shard_map/pallas_call | solution.py:48
  58.6 0.0 collective-permute-done.2.g1_ref.refs_1_
  58.6 0.0 copy-start.3
  58.6 0.0 copy-done
  58.6 0.7 copy-done.3
  59.4 11.5 %shard_map.62 = f32[64,128,128]{2,1,0:T(8,128)} custom-call(f32[4,64,256]{2,1,0:T(8,128)} %bitcast.23, f32[4,64,256]{2,1,0:T(8,128)} %copy-done.3, bf16[2,4,512,256]{3,2,1,0:T(8,128)(2,1)} %get-tuple-element.10.refs_2_.refs_6_.refs_7_.high_ref, bf16[2,4,512,256]{3,2,1,0:T(8,128)(2,1)} %get-tuple-element.11.refs_3_.refs_8_.refs_9_.low_ref), custom_call_target="tpu_custom_call" | custom-call | flops 3221225472 | bytes 6291456 | tf_op jit(solution)/shard_map/pallas_call | solution.py:132
  70.9 0.0 copy-start.1
  70.9 5.8 %all-to-all-start.3 = ((f32[64,128,128]{2,1,0:T(8,128)}), f32[64,128,128]{2,1,0:T(8,128)}, u32[]{:S(2)}, u32[]{:S(2)}) async-start(f32[64,128,128]{2,1,0:T(8,128)} %shard_map.62), calls=%async_computation.3 | async-start | bytes 8388608 | tf_op jit(solution)/shard_map/all_to_all | solution.py:413
  76.7 0.0 copy-done.1
  76.7 0.9 collective-permute-start
  77.6 96.5 %collective-permute-done.refs_0_.g2_ref = f32[4,64,256]{2,1,0:T(8,128)S(1)} collective-permute-done((f32[4,64,256]{2,1,0:T(8,128)S(1)}, f32[4,64,256]{2,1,0:T(8,128)S(1)}, u32[]{:S(2)}, u32[]{:S(2)}) %collective-permute-start) | collective-permute-done | bytes 262176 | tf_op jit(solution)/shard_map/ppermute | solution.py:396
  174.1 0.0 copy-start.4
  174.1 0.0 collective-permute-start.1
  174.1 1.5 collective-permute-done.1.refs_1_.g3_ref
  175.6 0.0 copy-done.4
  175.6 0.0 copy-start.5
  175.6 0.7 copy-done.5
  176.3 11.6 %shard_map.60 = f32[64,128,128]{2,1,0:T(8,128)} custom-call(f32[4,64,256]{2,1,0:T(8,128)} %copy-done.4, f32[4,64,256]{2,1,0:T(8,128)} %copy-done.5, bf16[2,4,512,256]{3,2,1,0:T(8,128)(2,1)} %get-tuple-element.10.refs_2_.refs_6_.refs_7_.high_ref, bf16[2,4,512,256]{3,2,1,0:T(8,128)(2,1)} %get-tuple-element.11.refs_3_.refs_8_.refs_9_.low_ref), custom_call_target="tpu_custom_call" | custom-call | flops 3221225472 | bytes 6291456 | tf_op jit(solution)/shard_map/pallas_call | solution.py:132
  187.9 0.0 all-to-all-done.3.refs_0_.refs_1_
  188.0 12.7 %all-to-all-start.2 = ((f32[64,128,128]{2,1,0:T(8,128)}), f32[64,128,128]{2,1,0:T(8,128)}, u32[]{:S(2)}, u32[]{:S(2)}) async-start(f32[64,128,128]{2,1,0:T(8,128)} %shard_map.60), calls=%async_computation.2 | async-start | bytes 8388608 | tf_op jit(solution)/shard_map/all_to_all | solution.py:413
  200.7 0.6 pad_add_fusion.row_ref.rows_ref
  201.2 0.6 pad_add_fusion.1.row_ref
  201.8 4.7 %shard_map.61 = (bf16[2,512,512]{2,1,0:T(8,128)(2,1)}, bf16[2,512,512]{2,1,0:T(8,128)(2,1)}, bf16[2,512,512]{2,1,0:T(8,128)(2,1)}, bf16[2,512,512]{2,1,0:T(8,128)(2,1)}) custom-call(s32[1]{0:T(128)} %bitcast.7.quarter_ref, f32[4,64,256]{2,1,0:T(8,128)} %bitcast.24, f32[4,64,256]{2,1,0:T(8,128)} %copy-done.3, f32[4,64,256]{2,1,0:T(8,128)} %copy-done.4, ...), custom_call_target="tpu_custom_call" | custom-call | flops 1073741824 | bytes 5242880 | tf_op jit(solution)/shard_map/pallas_call | solution.py:183
  206.6 13.5 %shard_map.66.dual_hbm = f32[64,128,128]{2,1,0:T(8,128)} custom-call(s32[2]{0:T(128)} %pad_add_fusion.row_ref.rows_ref, s32[2]{0:T(128)} %pair_ref.5, bf16[2,512,512]{2,1,0:T(8,128)(2,1)} %get-tuple-element.12.refs_2_.vh_ref, bf16[2,512,512]{2,1,0:T(8,128)(2,1)} %get-tuple-element.13.refs_3_.vl_ref, bf16[2,512,512]{2,1,0:T(8,128)(2,1)} %get-tuple-element.14.refs_4_.wh_ref, ...), custom_call_target="tpu_custom_call" | custom-call | flops 6442450944 | bytes 16777216 | tf_op jit(solution)/shard_map/pallas_call | solution.py:314
  220.1 0.6 broadcast_in_dim.16.refs_10_
  220.7 13.2 %shard_map.64 = (bf16[2,2,2,4,256,256]{5,4,3,2,1,0:T(8,128)(2,1)}, f32[64,128]{1,0:T(8,128)}) custom-call(s32[2]{0:T(128)} %pad_add_fusion.1.row_ref, s32[2]{0:T(128)} %pair_ref.5, f32[64,128,128]{2,1,0:T(8,128)} %all-to-all-done.3.refs_0_.refs_1_, f32[64,128,128]{2,1,0:T(8,128)} %all-to-all-done.3.refs_0_.refs_1_, ...), custom_call_target="tpu_custom_call", output_to_operand_aliasing={{0}: (13, {})} | custom-call | flops 6442450944 | bytes 20971520 | tf_op jit(solution)/shard_map/pallas_call | solution.py:265
  233.9 68.8 %all-to-all-done.2.refs_0_.refs_1_.got_hbm = f32[64,128,128]{2,1,0:T(8,128)} async-done(((f32[64,128,128]{2,1,0:T(8,128)}), f32[64,128,128]{2,1,0:T(8,128)}, u32[]{:S(2)}, u32[]{:S(2)}) %all-to-all-start.2) | async-done | bytes 4194336 | tf_op jit(solution)/shard_map/all_to_all | solution.py:413
  302.7 5.1 %shard_map.67 = f32[64,128]{1,0:T(8,128)} custom-call(f32[64,128,128]{2,1,0:T(8,128)} %all-to-all-done.2.refs_0_.refs_1_.got_hbm, f32[64,128,128]{2,1,0:T(8,128)} %shard_map.66.dual_hbm, f32[64,128]{1,0:T(8,128)} %get-tuple-element.17.sums_ref), custom_call_target="tpu_custom_call" | custom-call | flops 4194304 | bytes 8388608 | tf_op jit(solution)/shard_map/pallas_call | solution.py:364
  307.8 5.4 %all-to-all-start.4 = ((f32[64,1,128]{2,1,0:T(1,128)}), f32[64,1,128]{2,1,0:T(1,128)S(1)}, u32[]{:S(2)}, u32[]{:S(2)}) async-start(f32[64,1,128]{2,1,0:T(1,128)} %bitcast.26), calls=%async_computation.4 | async-start | bytes 65536 | tf_op jit(solution)/shard_map/all_to_all | solution.py:417
  313.2 10.8 %shard_map.65 = bf16[2,2,2,4,256,256]{5,4,3,2,1,0:T(8,128)(2,1)} custom-call(s32[2]{0:T(128)} %pad_add_fusion.row_ref.rows_ref, s32[2]{0:T(128)} %pair_ref.5, f32[64,128,128]{2,1,0:T(8,128)} %all-to-all-done.2.refs_0_.refs_1_.got_hbm, f32[64,128,128]{2,1,0:T(8,128)} %all-to-all-done.2.refs_0_.refs_1_.got_hbm, ...), custom_call_target="tpu_custom_call", output_to_operand_aliasing={{}: (8, {})} | custom-call | flops 6442450944 | bytes 20971520 | tf_op jit(solution)/shard_map/pallas_call | solution.py:265
  324.1 1.1 all-to-all-done.4
  325.2 0.7 mul.7
  (7 shorter events, 0.1 us)
Async XLA Ops:
  0.6 16.4 %copy-start.2 = (s32[2]{0:T(128)S(1)}, s32[2]{0:T(128)}, u32[]{:S(2)}) copy-start(s32[2]{0:T(128)} %param.6) | copy-start | bytes 28
  3.4 29.0 %all-to-all-start = ((f32[64,4,256]{2,1,0:T(4,128)}), f32[64,4,256]{2,1,0:T(4,128)S(1)}, u32[]{:S(2)}, u32[]{:S(2)}) async-start(f32[64,4,256]{2,1,0:T(4,128)} %bitcast.19), calls=%async_computation | async-start | bytes 524288 | tf_op jit(solution)/shard_map/all_to_all | solution.py:385
  51.2 7.4 %copy-start = (f32[64,4,256]{2,0,1:T(8,128)}, f32[64,4,256]{2,0,1:T(8,128)S(1)}, u32[]{:S(2)}) copy-start(f32[64,4,256]{2,0,1:T(8,128)S(1)} %copy.17) | copy-start | bytes 786436
  51.3 7.4 %collective-permute-start.2 = (f32[4,64,256]{2,1,0:T(8,128)S(1)}, f32[4,64,256]{2,1,0:T(8,128)S(1)}, u32[]{:S(2)}, u32[]{:S(2)}) collective-permute-start(f32[4,64,256]{2,1,0:T(8,128)S(1)} %bitcast.22), channel_id=1, source_target_pairs={{1,0},{0,1},{3,2},{2,3},{5,4},{4,5},{7,6},{6,7},{9,8},{8,9},{11,10... | collective-permute-start | bytes 786440 | tf_op jit(solution)/shard_map/ppermute | solution.py:395
  58.6 0.7 copy-start.3
  70.9 5.8 %copy-start.1 = (f32[64,4,256]{2,0,1:T(8,128)S(1)}, f32[64,4,256]{2,0,1:T(8,128)}, u32[]{:S(2)}) copy-start(f32[64,4,256]{2,0,1:T(8,128)} %copy-done) | copy-start | bytes 786436
  70.9 117.0 %all-to-all-start.3 = ((f32[64,128,128]{2,1,0:T(8,128)}), f32[64,128,128]{2,1,0:T(8,128)}, u32[]{:S(2)}, u32[]{:S(2)}) async-start(f32[64,128,128]{2,1,0:T(8,128)} %shard_map.62), calls=%async_computation.3 | async-start | bytes 8388608 | tf_op jit(solution)/shard_map/all_to_all | solution.py:413
  76.7 97.4 %collective-permute-start = (f32[4,64,256]{2,1,0:T(8,128)S(1)}, f32[4,64,256]{2,1,0:T(8,128)S(1)}, u32[]{:S(2)}, u32[]{:S(2)}) collective-permute-start(f32[4,64,256]{2,1,0:T(8,128)S(1)} %bitcast.25), channel_id=1, source_target_pairs={{2,0},{3,1},{0,2},{1,3},{6,4},{7,5},{4,6},{5,7},{10,8},{11,9},{8,1... | collective-permute-start | bytes 786440 | tf_op jit(solution)/shard_map/ppermute | solution.py:396
  174.1 1.5 copy-start.4
  174.1 1.5 collective-permute-start.1
  175.6 0.7 copy-start.5
  188.0 114.8 %all-to-all-start.2 = ((f32[64,128,128]{2,1,0:T(8,128)}), f32[64,128,128]{2,1,0:T(8,128)}, u32[]{:S(2)}, u32[]{:S(2)}) async-start(f32[64,128,128]{2,1,0:T(8,128)} %shard_map.60), calls=%async_computation.2 | async-start | bytes 8388608 | tf_op jit(solution)/shard_map/all_to_all | solution.py:413
  307.8 17.4 %all-to-all-start.4 = ((f32[64,1,128]{2,1,0:T(1,128)}), f32[64,1,128]{2,1,0:T(1,128)S(1)}, u32[]{:S(2)}, u32[]{:S(2)}) async-start(f32[64,1,128]{2,1,0:T(1,128)} %bitcast.26), calls=%async_computation.4 | async-start | bytes 65536 | tf_op jit(solution)/shard_map/all_to_all | solution.py:417
